TPU v7x, 32 devices: a whole 2x2x4 slice. The times are simulated.
32 devices in a mesh: batch: 4 (over x, core), hidden: 4 (over z), solver: 2 (over y).
Axes of the slice: x: 2, y: 2, z: 4, core: 2. Of those that a mesh axis runs over, the one named last changes fastest.
Arguments:
- activations: bfloat16 [1024, 4096], P('batch', ('hidden', 'solver')), may hold values from -16 to 16, as said below
- cotangent: bfloat16 [8192, 1024], P(('hidden', 'solver'), 'batch'), may hold values from -0.1875 to 0.1875
- weight: bfloat16 [4096, 8192], P(('hidden', 'solver'), 'batch'), may hold values from -0.09375 to 0.09375
- left_old: float32 [4, 8, 1024, 1024], P('hidden', 'batch'), may hold values from -0.001953125 to 2.0019531, as said below
- right_old: float32 [4, 8, 1024, 1024], P('hidden', 'batch'), may hold values from -0.001953125 to 2.0019531, as said below
Outputs:
- first_out: bfloat16 [8192, 1024], P(('hidden', 'solver'), 'batch')
- new_left: float32 [4, 8, 1024, 1024], P('hidden', 'batch', 'solver')
- new_right: float32 [4, 8, 1024, 1024], P('hidden', 'batch', 'solver')
- direction: float32 [4096, 8192], P(('hidden', 'solver'), 'batch')
- second_out: bfloat16 [8192, 1024], P(('hidden', 'solver'), 'batch')
Inputs may be any that keep to these rules, and one draw needn't show every extreme that they name: `activations`: in the hidden draw each feature carries its own scale. `left_old`: every block is symmetric, its diagonal is positive and larger than the sum of the magnitudes of the rest of its row. `right_old`: every block is symmetric, its diagonal is positive and larger than the sum of the magnitudes of the rest of its row.
All inputs are finite; a program needn't handle non-finite values. Where the computation divides by a largest or mean magnitude, that divisor is 1e-20 or more.
Results may differ from a plain program's by a relative error of at most 0.017.
Values may be sent and summed in bfloat16 or wider, within the bound.
A program may use at most 128 MiB of HBM per device.

v0:
```python
import jax
import jax.numpy as jnp
from jax import lax
from jax.sharding import PartitionSpec as P

BLOCK = 1024


STAT_DECAY = 0.8
LEARN_RATE = 0.005
EPSILON = 1e-06

ALL = ("batch", "hidden", "solver")
FEATURES = ("hidden", "solver")


def product(left_mat, right_mat):
    return jnp.einsum("bij,bjk->bik", left_mat, right_mat, preferred_element_type=jnp.float32)


def prepare(factor):
    identity = jnp.eye(BLOCK, dtype=jnp.float32)
    scaled = 2.5 / (jnp.max(jnp.sum(jnp.abs(factor), axis=2), axis=1) + EPSILON)
    moment = scaled[:, None, None] * factor
    newton_step = (5.0 * identity - moment) * 0.25
    return (scaled, moment.astype(jnp.bfloat16), newton_step.astype(jnp.bfloat16))


def apply_root(start, moment, step):
    power = start
    for _ in range(4):
        power = product(power.astype(jnp.bfloat16), step)
    power = product(power.astype(jnp.bfloat16), moment)
    return (5.0 * start.astype(jnp.float32) - power) * 0.25


def body(activations, cotangent, weight, left_old, right_old, *, n_batch, n_solver, n_feat):
    rows_here = weight.shape[0]
    nblocks = weight.shape[1] // BLOCK
    per_batch = n_feat // n_batch
    out_rows = weight.shape[1] // per_batch
    tokens = activations.shape[0]
    to_owner = [
        (b * n_feat + c * n_batch + t, t * n_feat + b * per_batch + c)
        for b in range(n_batch)
        for c in range(per_batch)
        for t in range(n_batch)
    ]
    from_owner = [(target, source) for source, target in to_owner]

    def partial_forward(weight_here):
        split = weight_here.reshape(rows_here, per_batch, out_rows)
        out = jnp.einsum("fco,btf->cbot", split, acts_all, preferred_element_type=jnp.float32)
        return out.astype(jnp.bfloat16).reshape(n_feat * out_rows, tokens)

    def reduce_forward(partial):
        return lax.psum_scatter(partial, FEATURES, scatter_dimension=0, tiled=True)

    acts_all = lax.all_gather(activations, "batch", axis=0, tiled=False)
    here = lax.axis_index("solver")
    acts_block = jnp.zeros((n_batch, tokens, n_solver * rows_here), acts_all.dtype)
    for shift in range(n_solver):
        part = acts_all
        if shift > 0:
            pairs = [(at, (at + shift) % n_solver) for at in range(n_solver)]
            part = lax.ppermute(acts_all, "solver", pairs)
        first_col = lax.rem(here + n_solver - shift, n_solver) * rows_here
        acts_block = lax.dynamic_update_slice_in_dim(acts_block, part, first_col, 2)
    cot_moved = lax.ppermute(cotangent, ALL, from_owner)
    cot_all = lax.all_gather(cot_moved, FEATURES, axis=0, tiled=False)
    cot_all = cot_all.reshape(per_batch, n_batch, out_rows, tokens)
    first_partial = partial_forward(weight)
    first_partial, cot_all = lax.optimization_barrier((first_partial, cot_all))
    first_sum = reduce_forward(first_partial)
    grad_full = jnp.einsum("cbot,btf->cof", cot_all, acts_block, preferred_element_type=jnp.float32)
    grad_full = grad_full.astype(jnp.bfloat16).reshape(nblocks, BLOCK, BLOCK)
    gram_left = jnp.einsum("bnm,bnk->bmk", grad_full, grad_full, preferred_element_type=jnp.float32)
    gram_right = jnp.einsum(
        "bnm,bkm->bnk", grad_full, grad_full, preferred_element_type=jnp.float32
    )
    left_all = STAT_DECAY * left_old[0] + (1.0 - STAT_DECAY) / BLOCK * gram_left
    right_all = STAT_DECAY * right_old[0] + (1.0 - STAT_DECAY) / BLOCK * gram_right
    first_row = lax.axis_index("solver") * rows_here
    new_left = lax.dynamic_slice_in_dim(left_all, first_row, rows_here, 1)[None]
    new_right = lax.dynamic_slice_in_dim(right_all, first_row, rows_here, 1)[None]
    scale_left, moment_left, step_left = prepare(left_all)
    own_rows = lax.dynamic_slice_in_dim(step_left, first_row, rows_here, 1)
    root_rows = apply_root(own_rows, moment_left, step_left)
    mixed_rows = jnp.einsum(
        "brm,bnm->brn",
        root_rows.astype(jnp.bfloat16),
        grad_full,
        preferred_element_type=jnp.float32,
    )
    scale_right, moment_right, step_right = prepare(right_all)
    turned = product(mixed_rows.astype(jnp.bfloat16), step_right)
    scale_both = (scale_left**0.25) * (scale_right**0.25)
    update = scale_both[:, None, None] * apply_root(turned, moment_right, step_right)
    update, first_sum = lax.optimization_barrier((update, first_sum))
    first_out = lax.ppermute(first_sum, ALL, to_owner)
    squares = lax.psum(jnp.sum(update * update, axis=(1, 2)), "solver")
    spread = jnp.sqrt(squares / (BLOCK * BLOCK) + EPSILON)
    scaled_update = update / spread[:, None, None]
    direction = jnp.transpose(scaled_update, (1, 0, 2)).reshape(rows_here, nblocks * BLOCK)
    new_weight = (weight.astype(jnp.float32) - LEARN_RATE * direction).astype(jnp.bfloat16)
    second_sum = reduce_forward(partial_forward(new_weight))
    second_sum, new_left, new_right = lax.optimization_barrier((second_sum, new_left, new_right))
    second_out = lax.ppermute(second_sum, ALL, to_owner)
    return (first_out, new_left, new_right, direction, second_out)


def solution(mesh):
    in_specs = (
        P("batch", ("hidden", "solver")),
        P(("hidden", "solver"), "batch"),
        P(("hidden", "solver"), "batch"),
        P("hidden", "batch", None, None),
        P("hidden", "batch", None, None),
    )
    out_specs = (
        P(("hidden", "solver"), "batch"),
        P("hidden", "batch", "solver", None),
        P("hidden", "batch", "solver", None),
        P(("hidden", "solver"), "batch"),
        P(("hidden", "solver"), "batch"),
    )
    n_batch = mesh.shape["batch"]
    n_feat = mesh.shape["hidden"] * mesh.shape["solver"]

    def step(activations, cotangent, weight, left_old, right_old):
        return body(
            activations,
            cotangent,
            weight,
            left_old,
            right_old,
            n_batch=n_batch,
            n_solver=mesh.shape["solver"],
            n_feat=n_feat,
        )

    return jax.shard_map(step, mesh=mesh, in_specs=in_specs, out_specs=out_specs, check_vma=False)
```

profile of v0, /device:TPU:4, one launch (start us, length us, event | category | flops | bytes accessed | tf_op | source)
XLA Modules:
  0.0 415.2 jit_solution(4227732098720041947)
XLA Ops:
  7.2 0.7 all-gather.5.cloned.1.call-update
  7.9 4.4 %collective-permute-start = (bf16[1024,256]{1,0:T(8,128)(2,1)}, bf16[1024,256]{1,0:T(8,128)(2,1)S(1)}, u32[]{:S(2)}, u32[]{:S(2)}) collective-permute-start(bf16[1024,256]{1,0:T(8,128)(2,1)} %param.6), channel_id=1, source_target_pairs={{0,0},{8,1},{16,2},{24,3},{1,4},{9,5},{17,6},{25,7},{2,8},{10,9},{... | collective-permute-start | bytes 1572872 | tf_op jit(solution)/shard_map/ppermute | solution.py:69
  12.4 12.1 %collective-permute-done = bf16[1024,256]{1,0:T(8,128)(2,1)S(1)} collective-permute-done((bf16[1024,256]{1,0:T(8,128)(2,1)}, bf16[1024,256]{1,0:T(8,128)(2,1)S(1)}, u32[]{:S(2)}, u32[]{:S(2)}) %collective-permute-start) | collective-permute-done | bytes 524320 | tf_op jit(solution)/shard_map/ppermute | solution.py:69
  24.5 0.8 copy-done.2
  25.4 0.0 reduce-scatter.3.cloned.1.call-start
  25.4 2.1 all-gather.5.cloned.1.call-done
  27.5 15.8 %collective-permute-start.1 = (bf16[4,256,512]{2,1,0:T(8,128)(2,1)}, bf16[4,256,512]{2,1,0:T(8,128)(2,1)}, u32[]{:S(2)}, u32[]{:S(2)}) collective-permute-start(bf16[4,256,512]{2,1,0:T(8,128)(2,1)} %bitcast.68), channel_id=1, source_target_pairs={{0,1},{1,0},{2,3},{3,2},{4,5},{5,4},{6,7},{7,6},{8,9},{9,8},{10,11... | collective-permute-start | bytes 3145736 | tf_op jit(solution)/shard_map/ppermute | solution.py:66
  43.2 8.7 %copy.35 = f32[1,2,1024,1024]{2,3,1,0:T(8,128)} copy(f32[1,2,1024,1024]{3,2,1,0:T(8,128)} %param.8) | data formatting | bytes 16777216 | tf_op args[3]
  51.9 8.8 %copy.47 = f32[1,2,1024,1024]{2,3,1,0:T(8,128)} copy(f32[1,2,1024,1024]{3,2,1,0:T(8,128)} %param.9) | data formatting | bytes 16777216 | tf_op args[4]
  60.7 2.5 fusion.4
  63.2 0.4 copy-done.1
  63.6 4.4 %convert_bitcast_fusion = bf16[2,4,1024,256]{2,3,0,1:T(8,128)(2,1)} fusion(bf16[4,256,512,1]{2,1,3,0:T(8,128)(2,1)S(1)} %bitcast.69, bf16[64,2,8,1024]{3,2,1,0:T(8,128)(2,1)S(1)} %bitcast.67), kind=kOutput, calls=%fused_computation.17 | convolution fusion | flops 2149580800 | bytes 7340032 | tf_op jit(solution)/shard_map/fco,btf->cbot/dot_general | solution.py:53
  68.0 6.3 %copy.37 = bf16[2,4,1024,256]{3,2,1,0:T(8,128)(2,1)} copy(bf16[2,4,1024,256]{2,3,0,1:T(8,128)(2,1)} %convert_bitcast_fusion) | data formatting | bytes 8388608 | tf_op jit(solution)/shard_map/convert_element_type | solution.py:54
  74.3 0.3 broadcast_in_dim.6
  74.5 0.2 constant_dynamic-update-slice_fusion.1
  74.7 1.4 constant_dynamic-update-slice_fusion
  76.1 47.6 %all-gather.7.cloned.1.call-done = bf16[8192,256]{1,0:T(8,128)(2,1)} async-done(((bf16[1024,256]{1,0:T(8,128)(2,1)}), bf16[8192,256]{1,0:T(8,128)(2,1)}) %all-gather.7.cloned.1.call-update) | async-done | bytes 4194320 | tf_op jit(solution)/shard_map/all_gather | solution.py:70
  123.7 0.2 reduce-scatter.5.cloned.1.call-start
  124.0 6.9 %bitcast_convert_fusion = bf16[2,1024,1024]{2,1,0:T(8,128)(2,1)S(1)} fusion(bf16[2,4,1024,256]{3,2,1,0:T(8,128)(2,1)} %bitcast.72, bf16[4,256,1024]{2,1,0:T(8,128)(2,1)S(1)} %constant_dynamic-update-slice_fusion), kind=kOutput, calls=%fused_computation.1 | convolution fusion | flops 4297064448 | bytes 10485760 | tf_op jit(solution)/shard_map/cbot,btf->cof/dot_general | solution.py:75
  130.9 11.6 %abs_reduce_fusion.1 = (f32[2,1024]{1,0:T(2,128)S(1)}, f32[2,1024,1024]{1,2,0:T(8,128)}) fusion(bf16[2,1024,1024]{2,1,0:T(8,128)(2,1)S(1)} %bitcast_convert_fusion, f32[1,2,1024,1024]{2,3,1,0:T(8,128)} %copy.35), kind=kOutput, calls=%fused_computation.6 | convolution fusion | flops 4305451008 | bytes 20979712 | tf_op jit(solution)/shard_map/bnm,bnk->bmk/dot_general | solution.py:77
  142.5 9.5 %abs_reduce_fusion = (f32[2,1024]{1,0:T(2,128)S(1)}, f32[2,1024,1024]{1,2,0:T(8,128)}) fusion(bf16[2,1024,1024]{2,1,0:T(8,128)(2,1)S(1)} %bitcast_convert_fusion, f32[1,2,1024,1024]{2,3,1,0:T(8,128)} %copy.47), kind=kOutput, calls=%fused_computation.4 | convolution fusion | flops 4305451008 | bytes 20979712 | tf_op jit(solution)/shard_map/bnm,bkm->bnk/dot_general | solution.py:78
  152.0 0.1 reduce_max.18
  152.2 0.1 reduce_max.19
  152.3 12.2 %multiply_convert_fusion.1 = (bf16[2,1024,1024]{1,2,0:T(8,128)(2,1)}, bf16[2,1024,1024]{1,2,0:T(8,128)(2,1)}) fusion(f32[2,1024,1024]{1,2,0:T(8,128)} %get-tuple-element.40, f32[2]{0:T(128)S(1)} %get-tuple-element.35, f32[1024,1024]{0,1:T(8,128)} %fusion.4, f32[2,1024,1024]{1,2,0:T(8,128)} %get-tuple-element.42, f32[2]{0:T(128)S(1)} %get-tuple-element.36), kind=kLoop, calls=%fused_computation.5 | loop fusion | flops 16777216 | bytes 29360144 | tf_op jit(solution)/shard_map/convert_element_type | solution.py:26
  164.5 10.1 %fusion.25 = bf16[2,512,1024]{2,1,0:T(8,128)(2,1)} fusion(bf16[2,1024,1024]{1,2,0:T(8,128)(2,1)} %get-tuple-element.37, s32[]{:T(128)S(6)} %select_n.13), kind=kOutput, calls=%fused_computation.43 | convolution fusion | flops 4296015872 | bytes 12582916 | tf_op jit(solution)/shard_map/bij,bjk->bik/dot_general | solution.py:18
  174.6 8.7 %fusion.21 = bf16[2,512,1024]{2,1,0:T(8,128)(2,1)S(1)} fusion(bf16[2,1024,1024]{1,2,0:T(8,128)(2,1)} %get-tuple-element.37, bf16[2,512,1024]{2,1,0:T(8,128)(2,1)} %fusion.25), kind=kOutput, calls=%fused_computation.39 | convolution fusion | flops 4296015872 | bytes 8388608 | tf_op jit(solution)/shard_map/bij,bjk->bik/dot_general | solution.py:18
  183.3 7.8 %fusion = f32[2,512,1024]{1,2,0:T(8,128)} fusion(f32[2,1024,1024]{1,2,0:T(8,128)} %get-tuple-element.40, f32[2]{0:T(128)S(1)} %get-tuple-element.35, bf16[2,512,1024]{2,1,0:T(8,128)(2,1)S(1)} %fusion.21), kind=kOutput, calls=%fused_computation.9 | convolution fusion | flops 2151677952 | bytes 14680072 | tf_op jit(solution)/shard_map/bij,bjk->bik/dot_general | solution.py:18
  191.1 12.6 %fusion.17 = f32[2,512,1024]{2,1,0:T(8,128)} fusion(bf16[2,1024,1024]{1,2,0:T(8,128)(2,1)} %get-tuple-element.38, bf16[2,1024,1024]{2,1,0:T(8,128)(2,1)} %copy-done.4, f32[2,512,1024]{1,2,0:T(8,128)} %fusion, bf16[2,1024,1024]{1,2,0:T(8,128)(2,1)} %get-tuple-element.37, s32[]{:T(128)S(6)} %select_n.13), kind=kOutput, calls=%fused_computation.35 | convolution fusion | flops 4301258752 | bytes 18874372 | tf_op jit(solution)/shard_map/bij,bjk->bik/dot_general | solution.py:18
  203.7 5.4 %copy.49 = f32[2,512,1024]{1,2,0:T(8,128)} copy(f32[2,512,1024]{2,1,0:T(8,128)} %fusion.17) | data formatting | bytes 8388608 | tf_op jit(solution)/shard_map/bij,bjk->bik/dot_general | solution.py:18
  209.1 10.6 %fusion.13 = bf16[2,512,1024]{2,1,0:T(8,128)(2,1)} fusion(bf16[2,1024,1024]{1,2,0:T(8,128)(2,1)} %get-tuple-element.38, f32[2,512,1024]{2,1,0:T(8,128)} %fusion.17), kind=kOutput, calls=%fused_computation.31 | convolution fusion | flops 4297064448 | bytes 10485760 | tf_op jit(solution)/shard_map/bij,bjk->bik/dot_general | solution.py:18
  219.7 8.6 %fusion.9 = bf16[2,512,1024]{2,1,0:T(8,128)(2,1)S(1)} fusion(bf16[2,1024,1024]{1,2,0:T(8,128)(2,1)} %get-tuple-element.38, bf16[2,512,1024]{2,1,0:T(8,128)(2,1)} %fusion.13), kind=kOutput, calls=%fused_computation.27 | convolution fusion | flops 4296015872 | bytes 8388608 | tf_op jit(solution)/shard_map/bij,bjk->bik/dot_general | solution.py:18
  228.3 9.0 %subtract_multiply_fusion = f32[2,512,1024]{1,2,0:T(8,128)} fusion(f32[2,512,1024]{1,2,0:T(8,128)} %copy.49, f32[2]{0:T(128)S(1)} %get-tuple-element.34, f32[2,1024,1024]{1,2,0:T(8,128)} %get-tuple-element.42, f32[2]{0:T(128)S(1)} %get-tuple-element.36, bf16[2,512,1024]{2,1,0:T(8,128)(2,1)S(1)} %fusion.9), kind=kOutput, calls=%fused_computation.13 | convolution fusion | flops 2154823680 | bytes 18874384 | tf_op jit(solution)/shard_map/bij,bjk->bik/dot_general | solution.py:18
  237.3 2.8 multiply_reduce_fusion
  240.1 4.9 %psum.7 = f32[2]{0:T(128)S(1)} all-reduce(f32[2]{0:T(128)S(1)} %multiply_reduce_fusion), channel_id=1, replica_groups=mesh['batch'=4,'hidden'=4,'solver'=2] {'solver'}, use_global_device_ids=true, to_apply=%region_6.0 | all-reduce | flops 2 | bytes 16 | tf_op jit(solution)/shard_map/psum | solution.py:101
  245.1 4.8 %broadcast_divide_fusion = f32[2,512,1024]{1,2,0:T(8,128)} fusion(f32[2,512,1024]{1,2,0:T(8,128)} %subtract_multiply_fusion, f32[2]{0:T(128)S(1)} %add_sqrt_fusion), kind=kLoop, calls=%fused_computation.25 | loop fusion | flops 1048576 | bytes 8388616 | tf_op jit(solution)/shard_map/div | solution.py:103
  249.9 5.5 %copy.56 = f32[512,2048]{1,0:T(8,128)} copy(f32[512,2048]{0,1:T(8,128)} %bitcast.62) | data formatting | bytes 8388608 | tf_op jit(solution)/shard_map/reshape | solution.py:104
  255.3 3.6 subtract_convert_fusion
  258.9 2.5 copy.80
  261.4 5.9 %convolution_convert_fusion = bf16[2,1024,4,256]{3,1,2,0:T(8,128)(2,1)} fusion(bf16[512,2,1024,1]{0,2,3,1:T(8,128)(2,1)} %bitcast.66, bf16[4,256,512,1]{2,1,0,3:T(8,128)(2,1)S(1)} %bitcast.71), kind=kOutput, calls=%fused_computation.20 | convolution fusion | flops 2149580800 | bytes 7340032 | tf_op jit(solution)/shard_map/fco,btf->cbot/dot_general | solution.py:53
  267.3 7.8 %constant_dynamic-slice_fusion = (f32[2,512,1024]{1,2,0:T(8,128)}, f32[2,512,1024]{1,2,0:T(8,128)}) fusion(f32[2,1024,1024]{1,2,0:T(8,128)} %get-tuple-element.42, s32[]{:T(128)S(6)} %select_n.13, f32[2,1024,1024]{1,2,0:T(8,128)} %get-tuple-element.40), kind=kLoop, calls=%fused_computation.50 | loop fusion | bytes 16777220 | tf_op jit(solution)/shard_map/dynamic_slice | solution.py:85
  275.2 5.3 %copy.59 = f32[2,512,1024]{2,1,0:T(8,128)} copy(f32[2,512,1024]{1,2,0:T(8,128)} %get-tuple-element.43) | data formatting | bytes 8388608 | tf_op jit(solution)/shard_map/dynamic_slice | solution.py:85
  280.5 5.4 %copy.58 = f32[2,512,1024]{2,1,0:T(8,128)} copy(f32[2,512,1024]{1,2,0:T(8,128)} %get-tuple-element.44) | data formatting | bytes 8388608 | tf_op jit(solution)/shard_map/dynamic_slice | solution.py:84
  285.9 1.9 collective-permute-start.2
  287.8 89.5 %reduce-scatter.5.cloned.1.call-done = bf16[1024,256]{1,0:T(8,128)(2,1)} async-done(((bf16[8192,256]{1,0:T(8,128)(2,1)}), bf16[1024,256]{1,0:T(8,128)(2,1)}) %reduce-scatter.5.cloned.1.call-update) | async-done | bytes 524304 | tf_op jit(solution)/shard_map/reduce_scatter | solution.py:57
  377.4 1.9 collective-permute-start.3
  379.3 27.6 %collective-permute-done.3 = bf16[1024,256]{1,0:T(8,128)(2,1)S(1)} collective-permute-done((bf16[1024,256]{1,0:T(8,128)(2,1)}, bf16[1024,256]{1,0:T(8,128)(2,1)S(1)}, u32[]{:S(2)}, u32[]{:S(2)}) %collective-permute-start.3) | collective-permute-done | bytes 524320 | tf_op jit(solution)/shard_map/ppermute | solution.py:108
  406.9 0.8 copy.90
  407.7 0.8 copy.91
  (18 shorter events, 0.2 us)
Async XLA Ops:
  7.2 20.3 %all-gather.5.cloned.1.call-start = ((), (), s32[]{:S(2)}) async-start(), calls=%async_computation.4 | async-start | bytes 1310720 | tf_op jit(solution)/shard_map/all_gather | solution.py:59
  7.9 115.8 %all-gather.7.cloned.1.call-start = ((), (), s32[]{:S(2)}) async-start(), calls=%async_computation.5 | async-start | bytes 4718592 | tf_op jit(solution)/shard_map/all_gather | solution.py:70
  7.9 16.6 %collective-permute-start = (bf16[1024,256]{1,0:T(8,128)(2,1)}, bf16[1024,256]{1,0:T(8,128)(2,1)S(1)}, u32[]{:S(2)}, u32[]{:S(2)}) collective-permute-start(bf16[1024,256]{1,0:T(8,128)(2,1)} %param.6), channel_id=1, source_target_pairs={{0,0},{8,1},{16,2},{24,3},{1,4},{9,5},{17,6},{25,7},{2,8},{10,9},{... | collective-permute-start | bytes 1572872 | tf_op jit(solution)/shard_map/ppermute | solution.py:69
  24.5 0.8 copy-start.2
  25.4 211.9 %reduce-scatter.3.cloned.1.call-start = ((), (), s32[]{:S(2)}) async-start(), calls=%async_computation.2 | async-start | bytes 4718592 | tf_op jit(solution)/shard_map/reduce_scatter | solution.py:57
  27.5 47.2 %collective-permute-start.1 = (bf16[4,256,512]{2,1,0:T(8,128)(2,1)}, bf16[4,256,512]{2,1,0:T(8,128)(2,1)}, u32[]{:S(2)}, u32[]{:S(2)}) collective-permute-start(bf16[4,256,512]{2,1,0:T(8,128)(2,1)} %bitcast.68), channel_id=1, source_target_pairs={{0,1},{1,0},{2,3},{3,2},{4,5},{5,4},{6,7},{7,6},{8,9},{9,8},{10,11... | collective-permute-start | bytes 3145736 | tf_op jit(solution)/shard_map/ppermute | solution.py:66
  60.7 2.5 copy-start
  60.7 2.9 copy-start.1
  123.7 253.6 %reduce-scatter.5.cloned.1.call-start = ((), (), s32[]{:S(2)}) async-start(), calls=%async_computation.3 | async-start | bytes 4718592 | tf_op jit(solution)/shard_map/reduce_scatter | solution.py:57
  130.9 11.6 %copy-start.4 = (bf16[2,1024,1024]{2,1,0:T(8,128)(2,1)}, bf16[2,1024,1024]{2,1,0:T(8,128)(2,1)S(1)}, u32[]{:S(2)}) copy-start(bf16[2,1024,1024]{2,1,0:T(8,128)(2,1)S(1)} %bitcast_convert_fusion) | copy-start | bytes 12582916
  280.5 5.4 %copy-start.3 = (bf16[1024,256]{1,0:T(8,128)(2,1)S(1)}, bf16[1024,256]{1,0:T(8,128)(2,1)}, u32[]{:S(2)}) copy-start(bf16[1024,256]{1,0:T(8,128)(2,1)} %reduce-scatter.3.cloned.1.call-done) | copy-start | bytes 1572868
  285.9 93.4 %collective-permute-start.2 = (bf16[1024,256]{1,0:T(8,128)(2,1)S(1)}, bf16[1024,256]{1,0:T(8,128)(2,1)S(1)}, u32[]{:S(2)}, u32[]{:S(2)}) collective-permute-start(bf16[1024,256]{1,0:T(8,128)(2,1)S(1)} %copy-done.3), channel_id=1, source_target_pairs={{0,0},{1,8},{2,16},{3,24},{4,1},{5,9},{6,17},{7,25},{8,2},{9,10},{... | collective-permute-start | bytes 1572872 | tf_op jit(solution)/shard_map/ppermute | solution.py:100
  377.4 29.6 %collective-permute-start.3 = (bf16[1024,256]{1,0:T(8,128)(2,1)}, bf16[1024,256]{1,0:T(8,128)(2,1)S(1)}, u32[]{:S(2)}, u32[]{:S(2)}) collective-permute-start(bf16[1024,256]{1,0:T(8,128)(2,1)} %reduce-scatter.5.cloned.1.call-done), channel_id=1, source_target_pairs={{0,0},{1,8},{2,16},{3,24},{4,1},{5,9},{6,17},{7,25},{8,2},{9,10},{... | collective-permute-start | bytes 1572872 | tf_op jit(solution)/shard_map/ppermute | solution.py:108
Sparse Core Ops, SparseCore 0:
  9.5 17.8 all-gather.4
  30.2 93.5 all-gather.6
  127.9 87.7 reduce-scatter.2
  267.5 109.8 reduce-scatter.4
where the time goes:
time: 420 us; the launch traced here: 415 us
  waiting for transfers between devices  180 us (43%)
  matrix products  106 us (25%)
  local copies, waits for them, and re-layouts  60.3 us (14%)
  other arithmetic  26.2 us (6%)
  starting transfers between devices  24.4 us (6%)
  between operations  14.1 us (3%)
  blocking collectives  4.92 us (1%)
    reduce_scatter x2, waiting for transfers between devices, reduce_forward(): return lax.psum_scatter(partial, FEATURES, scatter_dimension=0, tiled=True)  89.5 us
    dot_general x7, matrix products, product(): jnp.einsum('bij,bjk->bik', left_mat, right_mat, preferred_element_type=jn...  67.3 us
    all_gather x1, waiting for transfers between devices, body(): cot_all = lax.all_gather(cot_moved, FEATURES, axis=0, tiled=False)  47.6 us
    ppermute x1, waiting for transfers between devices, body(): second_out = lax.ppermute(second_sum, ALL, to_owner)  27.6 us
    unnamed x14, local copies, waits for them, and re-layouts  20.2 us
    ppermute x1, starting transfers between devices, body(): part = lax.ppermute(acts_all, 'solver', pairs)  15.8 us
    dynamic_slice x2, local copies, waits for them, and re-layouts, body(): lax.dynamic_slice_in_dim(right_all, first_row, rows_here, 1)[None]  13.1 us
    convert_element_type x1, other arithmetic, prepare(): newton_step.astype(jnp.bfloat16)  12.2 us
  transfers between devices with their start and end apart: 8, of which 5 were waited for; matrix products, arithmetic and copies ran while one was open for 40% of the time, Pallas kernels for 0%

commit v1 on v0

--- a/solution.py
+++ b/solution.py
@@ -1,6 +1,10 @@
+import functools
+
 import jax
 import jax.numpy as jnp
 from jax import lax
+from jax.experimental import pallas as pl
+from jax.experimental.pallas import tpu as pltpu
 from jax.sharding import PartitionSpec as P
 
 BLOCK = 1024
@@ -109,6 +113,656 @@
     return (first_out, new_left, new_right, direction, second_out)
 
 
+MESH = pl.DeviceIdType.MESH
+VMEM_LIMIT = 62 * 1024 * 1024
+PIECES = 4
+TILE = 256
+
+
+def remote(src, dst, send_sem, recv_sem, device):
+    return pltpu.make_async_remote_copy(
+        src_ref=src,
+        dst_ref=dst,
+        send_sem=send_sem,
+        recv_sem=recv_sem,
+        device_id=device,
+        device_id_type=MESH,
+    )
+
+
+def position():
+    return lax.axis_index("batch"), lax.axis_index("hidden"), lax.axis_index("solver")
+
+
+def flip(index, bits):
+    bit = 1
+    while bit <= bits:
+        if bits & bit:
+            index = index + bit * (1 - 2 * ((index // bit) % 2))
+        bit *= 2
+    return index
+
+
+def line_barrier(n_batch, n_line):
+    b, h, s = position()
+    barrier = pltpu.get_barrier_semaphore()
+    for bits in range(1, n_batch):
+        pl.semaphore_signal(barrier, inc=1, device_id=(flip(b, bits), h, s), device_id_type=MESH)
+    pl.semaphore_signal(barrier, inc=1, device_id=(b, h, 1 - s), device_id_type=MESH)
+
+    @pl.when(h > 0)
+    def _():
+        pl.semaphore_signal(barrier, inc=1, device_id=(b, h - 1, s), device_id_type=MESH)
+
+    @pl.when(h < n_line - 1)
+    def _():
+        pl.semaphore_signal(barrier, inc=1, device_id=(b, h + 1, s), device_id_type=MESH)
+
+    ends = (h == 0).astype(jnp.int32) + (h == n_line - 1).astype(jnp.int32)
+    pl.semaphore_wait(barrier, n_batch + 2 - ends)
+
+
+def gather_kernel(
+    n_batch,
+    n_line,
+    acts_ref,
+    cot_ref,
+    weight_ref,
+    grad_ref,
+    acts_all,
+    weight_all,
+    first_ref,
+    cot_line,
+    cot_all,
+    local_sem,
+    acts_send,
+    acts_recv,
+    weight_send,
+    weight_recv,
+    line_send,
+    line_recv,
+    swap_send,
+    swap_recv,
+    swap_local,
+):
+    b, h, s = position()
+    tokens, feats = acts_ref.shape
+    outs = cot_ref.shape[0]
+    rows = outs // PIECES
+
+    own_cot = pltpu.make_async_copy(cot_ref, cot_line.at[h], local_sem.at[0])
+
+    def acts_slot(bb, ss):
+        return acts_all.at[
+            pl.ds(pl.multiple_of(bb * tokens, tokens), tokens),
+            pl.ds(pl.multiple_of(ss * feats, feats), feats),
+        ]
+
+    def weight_from(ss):
+        return weight_ref.at[:, pl.ds(pl.multiple_of(ss * outs, outs), outs)]
+
+    def weight_slot(ss):
+        return weight_all.at[pl.ds(pl.multiple_of(ss * feats, feats), feats), :]
+
+    own_acts = pltpu.make_async_copy(acts_ref, acts_slot(b, s), local_sem.at[1])
+    own_weight = pltpu.make_async_copy(weight_from(s), weight_slot(s), local_sem.at[2])
+    own_cot.start()
+    own_acts.start()
+    own_weight.start()
+    line_barrier(n_batch, n_line)
+    own_acts.wait()
+    own_cot.wait()
+
+    def line_slot(hp, q):
+        return cot_line.at[hp, pl.ds(q * rows, rows)]
+
+    def up(hp, q):
+        return remote(
+            line_slot(hp, q), line_slot(hp, q), line_send.at[0, hp, q], line_recv.at[hp, q], (b, h + 1, s)
+        )
+
+    def down(hp, q):
+        return remote(
+            line_slot(hp, q), line_slot(hp, q), line_send.at[1, hp, q], line_recv.at[hp, q], (b, h - 1, s)
+        )
+
+    def swap_slot(bb, q):
+        return cot_all.at[pl.ds(q * rows, rows), pl.ds(pl.multiple_of(bb * tokens, tokens), tokens)]
+
+    def swap(hp, q):
+        return remote(
+            line_slot(hp, q), swap_slot(b, q), swap_send.at[hp, q], swap_recv.at[b, q], (hp, h, s)
+        )
+
+    def swap_here(q):
+        return pltpu.make_async_copy(line_slot(b, q), swap_slot(b, q), swap_local.at[q])
+
+    def pass_on(hp, q):
+        @pl.when(hp == b)
+        def _():
+            swap_here(q).start()
+
+        @pl.when(hp != b)
+        def _():
+            swap(hp, q).start()
+
+    far = n_batch // 2
+    acts_moves = []
+
+    def acts_move(bb, ss, device):
+        index = len(acts_moves)
+        move = remote(
+            acts_slot(bb, ss), acts_slot(bb, ss), acts_send.at[index], acts_recv.at[bb, ss], device
+        )
+        move.start()
+        acts_moves.append(move)
+
+    def acts_wait(bb, ss):
+        remote(acts_slot(bb, ss), acts_slot(bb, ss), acts_send.at[0], acts_recv.at[bb, ss], (b, h, s)).wait_recv()
+
+    acts_move(b, s, (flip(b, far), h, s))
+    acts_move(b, s, (b, h, 1 - s))
+    for q in range(PIECES):
+        @pl.when(h < n_line - 1)
+        def _():
+            up(h, q).start()
+
+        @pl.when(h > 0)
+        def _():
+            down(h, q).start()
+
+    near = [bits for bits in range(1, far)]
+    for bits in near:
+        acts_move(b, s, (flip(b, bits), h, s))
+    for q in range(PIECES):
+        pass_on(h, q)
+    acts_wait(flip(b, far), s)
+    acts_move(flip(b, far), s, (b, h, 1 - s))
+    for bits in near:
+        acts_move(flip(b, far), s, (flip(b, bits), h, s))
+    weight_move = remote(weight_from(1 - s), weight_slot(s), weight_send, weight_recv, (b, h, 1 - s))
+    weight_move.start()
+    for place in (b, flip(b, far)):
+        acts_wait(place, 1 - s)
+        for bits in near:
+            acts_move(place, 1 - s, (flip(b, bits), h, s))
+
+    for distance in range(1, n_line):
+        for q in range(PIECES):
+            @pl.when(h >= distance)
+            def _():
+                hp = h - distance
+                up(hp, q).wait_recv()
+
+                @pl.when(h < n_line - 1)
+                def _():
+                    up(hp, q).start()
+
+                pass_on(hp, q)
+
+            @pl.when(h + distance < n_line)
+            def _():
+                hp = h + distance
+                down(hp, q).wait_recv()
+
+                @pl.when(h > 0)
+                def _():
+                    down(hp, q).start()
+
+                pass_on(hp, q)
+
+    for bits in near:
+        for place in (flip(b, bits), flip(b, bits + far)):
+            for ss in range(2):
+                acts_wait(place, ss)
+    own_weight.wait()
+    weight_move.wait_recv()
+
+    def first_tile(i, carry):
+        at = pl.ds(pl.multiple_of(i * TILE, TILE), TILE)
+        first_ref[at, :] = jnp.dot(
+            acts_all[at, :], weight_all[...], preferred_element_type=jnp.float32
+        ).astype(jnp.bfloat16)
+        return carry
+
+    lax.fori_loop(0, acts_all.shape[0] // TILE, first_tile, 0)
+
+    for q in range(PIECES):
+        swap_here(q).wait()
+        for bits in range(1, n_batch):
+            place = flip(b, bits)
+            remote(
+                swap_slot(place, q), swap_slot(place, q), swap_send.at[0, q], swap_recv.at[place, q], (b, h, s)
+            ).wait_recv()
+
+    def grad_tile(i, carry):
+        at = pl.ds(pl.multiple_of(i * TILE, TILE), TILE)
+        grad_ref[at, :] = jnp.dot(
+            cot_all[at, :], acts_all[...], preferred_element_type=jnp.float32
+        ).astype(jnp.bfloat16)
+        return carry
+
+    lax.fori_loop(0, outs // TILE, grad_tile, 0)
+
+    for move in acts_moves:
+        move.wait_send()
+    weight_move.wait_send()
+    for hp in range(n_line):
+        for q in range(PIECES):
+            @pl.when((hp <= h) & (h < n_line - 1))
+            def _():
+                up(hp, q).wait_send()
+
+            @pl.when((hp >= h) & (h > 0))
+            def _():
+                down(hp, q).wait_send()
+
+            @pl.when(hp != b)
+            def _():
+                swap(hp, q).wait_send()
+
+
+def gather(activations, cotangent, weight, n_batch, n_line):
+    tokens, feats = activations.shape
+    outs = cotangent.shape[0]
+    all_tokens, block = n_batch * tokens, 2 * feats
+    vmem = pl.BlockSpec(memory_space=pltpu.VMEM)
+    sem = pltpu.SemaphoreType.DMA
+    bf = jnp.bfloat16
+    return pl.pallas_call(
+        functools.partial(gather_kernel, n_batch, n_line),
+        out_shape=(
+            jax.ShapeDtypeStruct((outs, block), bf),
+            jax.ShapeDtypeStruct((all_tokens, block), bf),
+            jax.ShapeDtypeStruct((block, outs), bf),
+            jax.ShapeDtypeStruct((all_tokens, outs), bf),
+        ),
+        in_specs=[pl.BlockSpec(memory_space=pl.ANY)] * 3,
+        out_specs=(vmem,) * 4,
+        scratch_shapes=[
+            pltpu.VMEM((n_line, outs, tokens), bf),
+            pltpu.VMEM((outs, all_tokens), bf),
+            sem((3,)),
+            sem((2 * n_batch - 1,)),
+            sem((n_batch, 2)),
+            sem,
+            sem,
+            sem((2, n_line, PIECES)),
+            sem((n_line, PIECES)),
+            sem((n_line, PIECES)),
+            sem((n_batch, PIECES)),
+            sem((PIECES,)),
+        ],
+        compiler_params=pltpu.CompilerParams(
+            collective_id=0, has_side_effects=True, vmem_limit_bytes=VMEM_LIMIT
+        ),
+        name="gather",
+    )(activations, cotangent, weight)
+
+
+def tiles(count, step):
+    lax.fori_loop(0, count, lambda i, carry: (step(i), carry)[1], 0)
+
+
+def rows_at(i, size=TILE):
+    return pl.ds(pl.multiple_of(i * size, size), size)
+
+
+def dot(left, right):
+    return jnp.dot(left, right, preferred_element_type=jnp.float32)
+
+
+def update_statistics(old, left, right, own, sent, worst, s):
+    half = old.shape[0] // 2
+    worst[...] = jnp.zeros_like(worst)
+
+    def step(i):
+        at = rows_at(i)
+        new = STAT_DECAY * old[at, :] + (1.0 - STAT_DECAY) / BLOCK * dot(left[at, :], right[...])
+        old[at, :] = new
+        worst[...] = jnp.maximum(
+            worst[...], jnp.max(jnp.sum(jnp.abs(new), axis=1, keepdims=True), axis=0, keepdims=True)
+        )
+
+    tiles(old.shape[0] // TILE, step)
+
+    def split(i):
+        here = rows_at(i)
+        first = pl.multiple_of(s * half + i * TILE, TILE)
+        other = pl.multiple_of((1 - s) * half + i * TILE, TILE)
+        own[here, :] = old[pl.ds(first, TILE), :]
+        sent[here, :] = old[pl.ds(other, TILE), :].astype(jnp.bfloat16)
+
+    tiles(half // TILE, split)
+
+
+def series(stat, worst, step_one, step_two, step_three, tail):
+    size = stat.shape[0]
+    scaled = 2.5 / (worst[...] + EPSILON)
+
+    def first(i):
+        at = rows_at(i)
+        row = lax.broadcasted_iota(jnp.int32, (TILE, size), 0) + i * TILE
+        col = lax.broadcasted_iota(jnp.int32, (TILE, size), 1)
+        diagonal = jnp.where(row == col, 0.25, 0.0)
+        step_one[at, :] = (diagonal - (0.25 * scaled) * stat[at, :]).astype(jnp.bfloat16)
+
+    tiles(size // TILE, first)
+
+    def second(i):
+        at = rows_at(i)
+        two = dot(step_one[at, :], step_one[...])
+        two_low = two.astype(jnp.bfloat16)
+        three = dot(two_low, step_one[...])
+        step_two[at, :] = two_low
+        step_three[at, :] = three.astype(jnp.bfloat16)
+        tail[at, :] = (8.75 * step_one[at, :].astype(jnp.float32) + 4.75 * two + three).astype(jnp.bfloat16)
+
+    tiles(size // TILE, second)
+    return jnp.sqrt(jnp.sqrt(scaled))
+
+
+def root_rows(at, step_one, step_two, step_three, tail):
+    f32 = jnp.float32
+    return (
+        step_one[at, :].astype(f32)
+        + 2.5 * step_two[at, :].astype(f32)
+        + 7.5 * step_three[at, :].astype(f32)
+        + dot(step_three[at, :], tail[...])
+    ).astype(jnp.bfloat16)
+
+
+def block_kernel(
+    grad_ref,
+    acts_ref,
+    weight_ref,
+    left_ref,
+    right_ref,
+    left_own,
+    left_sent,
+    right_own,
+    right_sent,
+    direction_own,
+    direction_sent,
+    second_ref,
+    left,
+    right,
+    turned,
+    one,
+    two,
+    three,
+    tail,
+    root,
+    update,
+    worst,
+    squares,
+    sems,
+):
+    s = lax.axis_index("solver")
+    left_in = pltpu.make_async_copy(left_ref.at[0, s], left, sems.at[0])
+    right_in = pltpu.make_async_copy(right_ref.at[0, s], right, sems.at[1])
+    left_in.start()
+    right_in.start()
+
+    def turn(i):
+        turned[:, rows_at(i)] = grad_ref[rows_at(i), :].T
+
+    for i in range(grad_ref.shape[0] // TILE):
+        turn(i)
+
+    right_in.wait()
+    update_statistics(right, grad_ref, turned, right_own, right_sent, worst, s)
+    scale_right = series(right, worst, one, two, three, tail)
+
+    def right_root(i):
+        root[rows_at(i), :] = root_rows(rows_at(i), one, two, three, tail)
+
+    tiles(BLOCK // TILE, right_root)
+
+    left_in.wait()
+    update_statistics(left, turned, grad_ref, left_own, left_sent, worst, s)
+    scale = series(left, worst, one, two, three, tail) * scale_right
+    squares[...] = jnp.zeros_like(squares)
+
+    def apply(i):
+        at = rows_at(i)
+        left_rows = root_rows(at, one, two, three, tail)
+        mixed = turned[at, :].astype(jnp.float32) + dot(left_rows, turned[...])
+        value = mixed + dot(mixed.astype(jnp.bfloat16), root[...])
+        update[at, :] = value
+        squares[...] += jnp.sum(jnp.sum(value * value, axis=1, keepdims=True), axis=0, keepdims=True)
+
+    tiles(BLOCK // TILE, apply)
+    scaled = scale / jnp.sqrt(scale * scale * squares[...] / (BLOCK * BLOCK) + EPSILON)
+    half = BLOCK // 2
+
+    def finish(i):
+        at = rows_at(i)
+        root[at, :] = (
+            weight_ref[at, :].astype(jnp.float32) - LEARN_RATE * (scaled * update[at, :])
+        ).astype(jnp.bfloat16)
+
+    tiles(BLOCK // TILE, finish)
+
+    def forward(i):
+        at = rows_at(i)
+        second_ref[at, :] = dot(acts_ref[at, :], root[...]).astype(jnp.bfloat16)
+
+    tiles(acts_ref.shape[0] // TILE, forward)
+
+    def split(i):
+        here = rows_at(i)
+        first = pl.multiple_of(s * half + i * TILE, TILE)
+        other = pl.multiple_of((1 - s) * half + i * TILE, TILE)
+        direction_own[here, :] = scaled * update[pl.ds(first, TILE), :]
+        direction_sent[here, :] = (scaled * update[pl.ds(other, TILE), :]).astype(jnp.bfloat16)
+
+    tiles(half // TILE, split)
+
+
+def block_step(grad, acts, weight, left_old, right_old):
+    f32, bf = jnp.float32, jnp.bfloat16
+    half = BLOCK // 2
+    vmem = pl.BlockSpec(memory_space=pltpu.VMEM)
+    hbm = pl.BlockSpec(memory_space=pl.ANY)
+    own, sent = jax.ShapeDtypeStruct((half, BLOCK), f32), jax.ShapeDtypeStruct((half, BLOCK), bf)
+    low = pltpu.VMEM((BLOCK, BLOCK), bf)
+    wide = pltpu.VMEM((BLOCK, BLOCK), f32)
+    return pl.pallas_call(
+        block_kernel,
+        out_shape=(own, sent, own, sent, own, sent, jax.ShapeDtypeStruct(acts.shape, bf)),
+        in_specs=[vmem] * 3 + [hbm] * 2,
+        out_specs=(vmem,) * 7,
+        scratch_shapes=[
+            wide,
+            wide,
+            low,
+            low,
+            low,
+            low,
+            low,
+            low,
+            wide,
+            pltpu.VMEM((1, 1), f32),
+            pltpu.VMEM((1, 1), f32),
+            pltpu.SemaphoreType.DMA((2,)),
+        ],
+        compiler_params=pltpu.CompilerParams(vmem_limit_bytes=VMEM_LIMIT),
+        name="block_step",
+    )(grad, acts, weight, left_old, right_old)
+
+
+def scatter_kernel(n_batch, n_line, *refs):
+    partials, sent = refs[0:2], refs[2:5]
+    outs, got = refs[5:7], refs[7:10]
+    inbox, from_above, from_below = refs[10:13]
+    side_send, side_recv, local, swap_send, swap_recv, line_send, line_recv = refs[13:]
+    b, h, s = position()
+    tokens = outs[0].shape[0]
+    rows = tokens // PIECES
+
+    line_barrier(n_batch, n_line)
+
+    def piece(p, bb, q):
+        return inbox.at[p, bb, pl.ds(q * rows, rows)]
+
+    def outgoing(p, bb, q):
+        return partials[p].at[pl.ds(pl.multiple_of(bb * tokens + q * rows, rows), rows)]
+
+    def own(p, q):
+        return pltpu.make_async_copy(outgoing(p, b, q), piece(p, b, q), local.at[p, q])
+
+    def swap(p, bits, q):
+        to = flip(b, bits)
+        return remote(
+            outgoing(p, to, q), piece(p, b, q), swap_send.at[p, bits, q], swap_recv.at[p, bits, q], (to, h, s)
+        )
+
+    def down(p, bb, q):
+        at = pl.ds(q * rows, rows)
+        return (from_above.at[p, bb, at], line_send.at[p, bb, q], line_recv.at[p, 0, bb, q], (b, h - 1, s))
+
+    def up(p, bb, q):
+        at = pl.ds(q * rows, rows)
+        return (from_below.at[p, bb, at], line_send.at[p, bb, q], line_recv.at[p, 1, bb, q], (b, h + 1, s))
+
+    def line(how, p, bb, q, first):
+        slot, send, recv, device = how(p, bb, q)
+        return remote(piece(p, bb, q) if first else slot, slot, send, recv, device)
+
+    def add(slot, p, bb, q):
+        slot[...] = (slot[...].astype(jnp.float32) + piece(p, bb, q)[...].astype(jnp.float32)).astype(slot.dtype)
+
+    side = [
+        remote(sent[i], got[i], side_send.at[i], side_recv.at[i], (b, h, 1 - s)) for i in range(len(sent))
+    ]
+    order = [n_batch // 2 + bits for bits in range(n_batch // 2)] + list(range(1, n_batch // 2))
+    for p in range(len(partials)):
+        for q in range(PIECES):
+            own(p, q).start()
+        for bits in order:
+            for q in range(PIECES):
+                swap(p, bits, q).start()
+        if p == 0:
+            for move in side:
+                move.start()
+
+    for p in range(len(partials)):
+        for bits in range(n_batch):
+            bb = flip(b, bits)
+            for q in range(PIECES):
+                if bits == 0:
+                    own(p, q).wait()
+                else:
+                    swap(p, bits, q).wait_recv()
+
+                def forward(how, first):
+                    @pl.when(first)
+                    def _():
+                        line(how, p, bb, q, True).start()
+
+                    @pl.when(jnp.logical_not(first))
+                    def _():
+                        line(how, p, bb, q, False).wait_recv()
+                        add(how(p, bb, q)[0], p, bb, q)
+                        line(how, p, bb, q, False).start()
+
+                @pl.when(bb < h)
+                def _():
+                    forward(down, h == n_line - 1)
+
+                @pl.when(bb > h)
+                def _():
+                    forward(up, h == 0)
+
+        for q in range(PIECES):
+            at = pl.ds(q * rows, rows)
+            outs[p][at, :] = piece(p, h, q)[...]
+
+            @pl.when(h < n_line - 1)
+            def _():
+                line(down, p, h, q, False).wait_recv()
+                outs[p][at, :] = (
+                    outs[p][at, :].astype(jnp.float32) + from_above[p, h, at].astype(jnp.float32)
+                ).astype(outs[p].dtype)
+
+            @pl.when(h > 0)
+            def _():
+                line(up, p, h, q, False).wait_recv()
+                outs[p][at, :] = (
+                    outs[p][at, :].astype(jnp.float32) + from_below[p, h, at].astype(jnp.float32)
+                ).astype(outs[p].dtype)
+
+    for p in range(len(partials)):
+        for q in range(PIECES):
+            for bits in range(1, n_batch):
+                swap(p, bits, q).wait_send()
+            for bb in range(n_line):
+                @pl.when(h > bb)
+                def _():
+                    line(down, p, bb, q, False).wait_send()
+
+                @pl.when(h < bb)
+                def _():
+                    line(up, p, bb, q, False).wait_send()
+
+    for move in side:
+        move.wait()
+
+
+def scatter(partials, sent, n_batch, n_line):
+    all_tokens, width = partials[0].shape
+    tokens = all_tokens // n_batch
+    vmem = pl.BlockSpec(memory_space=pltpu.VMEM)
+    hbm = pl.BlockSpec(memory_space=pl.ANY)
+    sem = pltpu.SemaphoreType.DMA
+    bf = jnp.bfloat16
+    many = len(partials)
+    return pl.pallas_call(
+        functools.partial(scatter_kernel, n_batch, n_line),
+        out_shape=tuple(jax.ShapeDtypeStruct((tokens, width), bf) for _ in partials)
+        + tuple(jax.ShapeDtypeStruct(part.shape, part.dtype) for part in sent),
+        in_specs=[hbm] * (many + len(sent)),
+        out_specs=(vmem,) * many + (hbm,) * len(sent),
+        scratch_shapes=[
+            pltpu.VMEM((many, n_batch, tokens, width), bf),
+            pltpu.VMEM((many, n_line, tokens, width), bf),
+            pltpu.VMEM((many, n_line, tokens, width), bf),
+            sem((len(sent),)),
+            sem((len(sent),)),
+            sem((many, PIECES)),
+            sem((many, n_batch, PIECES)),
+            sem((many, n_batch, PIECES)),
+            sem((many, n_line, PIECES)),
+            sem((many, 2, n_line, PIECES)),
+        ],
+        compiler_params=pltpu.CompilerParams(
+            collective_id=1, has_side_effects=True, vmem_limit_bytes=VMEM_LIMIT
+        ),
+        name="scatter",
+    )(*partials, *sent)
+
+
+def owned_body(activations, cotangent, weight, left_old, right_old, *, n_batch, n_line):
+    s = lax.axis_index("solver")
+    grad, acts, block_weight, first_partial = gather(activations, cotangent, weight, n_batch, n_line)
+    left_own, left_sent, right_own, right_sent, direction_own, direction_sent, second_partial = block_step(
+        grad, acts, block_weight, left_old, right_old
+    )
+    first, second, left_got, right_got, direction_got = scatter(
+        (first_partial, second_partial), (left_sent, right_sent, direction_sent), n_batch, n_line
+    )
+
+    def joined(own, got, axis):
+        got = got.astype(jnp.float32)
+        return jnp.where(s == 0, jnp.stack([own, got], axis), jnp.stack([got, own], axis))
+
+    new_left = joined(left_own, left_got, 0)[None]
+    new_right = joined(right_own, right_got, 0)[None]
+    direction = joined(direction_own, direction_got, 1).reshape(direction_own.shape[0], -1)
+    return (first.T, new_left, new_right, direction, second.T)
+
+
 def solution(mesh):
     in_specs = (
         P("batch", ("hidden", "solver")),
@@ -127,7 +781,18 @@
     n_batch = mesh.shape["batch"]
     n_feat = mesh.shape["hidden"] * mesh.shape["solver"]
 
+    n_line = mesh.shape["hidden"]
+    n_solver = mesh.shape["solver"]
+
+    def owned(activations, cotangent, weight, left_old, right_old):
+        blocks = left_old.shape[1]
+        even = n_line == n_batch and n_batch & (n_batch - 1) == 0 and n_batch > 2
+        return even and n_solver == 2 and blocks == n_solver and cotangent.shape[0] == BLOCK
+
     def step(activations, cotangent, weight, left_old, right_old):
+        args = (activations, cotangent, weight, left_old, right_old)
+        if owned(*args):
+            return owned_body(*args, n_batch=n_batch, n_line=n_line)
         return body(
             activations,
             cotangent,

time: 420 us -> 221 us (0.53)
  the two profiles are of different devices: /device:TPU:4 before, /device:TPU:24 now
where the time goes in v1:
time: 221 us; the launch traced here: 218 us
  Pallas kernels  187 us (85%)
  other arithmetic  15.4 us (7%)
  local copies, waits for them, and re-layouts  14.2 us (6%)
    pallas_call x1, Pallas kernels, scatter(): pl.pallas_call(functools.partial(scatter_kernel, n_batch, n_line), out_sh...  91.1 us
    pallas_call x1, Pallas kernels, gather(): pl.pallas_call(functools.partial(gather_kernel, n_batch, n_line), out_sha...  50.3 us
    pallas_call x1, Pallas kernels, block_step(): pl.pallas_call(block_kernel, out_shape=(own, sent, own, sent, own, sent,...  46 us
    select_n x3, other arithmetic, joined(): jnp.where(s == 0, jnp.stack([own, got], axis), jnp.stack([got, own], axis))  11.9 us
    unnamed x11, local copies, waits for them, and re-layouts  8.87 us
    select_n x1, local copies, waits for them, and re-layouts, joined(): jnp.where(s == 0, jnp.stack([own, got], axis), jnp.stack([got, own], axis))  5.35 us

profile of v1, /device:TPU:24, one launch (start us, length us, event | category | flops | bytes accessed | tf_op | source)
XLA Modules:
  0.0 217.8 jit_solution(7678403816679748932)
XLA Ops:
  0.6 50.3 %gather.1 = (bf16[1024,1024]{1,0:T(8,128)(2,1)}, bf16[1024,1024]{1,0:T(8,128)(2,1)}, bf16[1024,1024]{1,0:T(8,128)(2,1)}, bf16[1024,1024]{1,0:T(8,128)(2,1)}) custom-call(bf16[256,512]{1,0:T(8,128)(2,1)} %acts_ref.1, bf16[1024,256]{1,0:T(8,128)(2,1)} %cot_ref.1, bf16[512,2048]{1,0:T(8,128)(2,1)} %weight_ref.1), custom_call_target="tpu_custom_call" | custom-call | tf_op jit(solution)/shard_map/gather/pallas_call | solution.py:372
  51.0 46.0 %block_step.1 = (f32[512,1024]{1,0:T(8,128)}, bf16[512,1024]{1,0:T(8,128)(2,1)}, f32[512,1024]{1,0:T(8,128)}, bf16[512,1024]{1,0:T(8,128)(2,1)}, f32[512,1024]{1...) custom-call(bf16[1024,1024]{1,0:T(8,128)(2,1)} %get-tuple-element.22.grad_ref, ...), custom_call_target="tpu_custom_call" | custom-call | tf_op jit(solution)/shard_map/block_step/pallas_call | solution.py:571
  97.0 91.1 %scatter.1 = (bf16[256,1024]{1,0:T(8,128)(2,1)}, bf16[256,1024]{1,0:T(8,128)(2,1)}, bf16[512,1024]{1,0:T(8,128)(2,1)}, bf16[512,1024]{1,0:T(8,128)(2,1)}, bf16[512,1024]{1,0:T(8,128)(2,1)}) custom-call(bf16[1024,1024]{1,0:T(8,128)(2,1)} %get-tuple-element.21.refs_0_, bf16[1024,1024]{1,0:T(8,128)(2,1)} %get-tuple-element.25.refs_1_, ...), custom_call_target="tpu_custom_call" | custom-call | tf_op jit(solution)/shard_map/scatter/pallas_call | solution.py:721
  188.1 2.0 copy.13
  190.2 3.3 %bitcast_convert_fusion.1 = (f32[1,1,512,1024]{3,2,1,0:T(8,128)S(1)}, f32[1,1,512,1024]{3,2,1,0:T(8,128)}) fusion(bf16[512,1024]{1,0:T(8,128)(2,1)} %get-tuple-element.33, bf16[512,1024]{1,0:T(8,128)(2,1)} %get-tuple-element.31), kind=kLoop, calls=%fused_computation.4 | loop fusion | flops 1048576 | bytes 6291456 | tf_op jit(solution)/shard_map/stack | solution.py:758
  193.4 0.0 copy-start.1
  193.4 7.0 %maximum_select_fusion = f32[1,2,512,1024]{3,2,1,0:T(8,128)} fusion(f32[1,1,512,1024]{3,2,1,0:T(8,128)} %get-tuple-element.48, f32[1,1,512,1024]{3,2,1,0:T(8,128)} %bitcast.18, pred[]{:T(512)S(6)} %eq.2), kind=kLoop, calls=%fused_computation | loop fusion | flops 3145728 | bytes 8388609 | tf_op jit(solution)/shard_map/jit(_where)/select_n | solution.py:758
  200.4 0.0 copy-done.1
  200.4 0.0 copy-start.2
  200.4 0.0 copy-start
  200.5 2.5 %maximum_select_fusion.1 = f32[1,2,512,1024]{3,2,1,0:T(8,128)} fusion(f32[1,1,512,1024]{3,2,1,0:T(8,128)S(1)} %get-tuple-element.47, f32[1,1,512,1024]{3,2,1,0:T(8,128)S(1)} %bitcast.17, pred[]{:T(512)S(6)} %eq.2), kind=kLoop, calls=%fused_computation.1 | loop fusion | flops 3145728 | bytes 8388609 | tf_op jit(solution)/shard_map/jit(_where)/select_n | solution.py:758
  202.9 0.0 copy-done.2
  202.9 0.2 bitcast_convert_fusion
  203.2 0.4 copy-done
  203.6 2.5 %maximum_select_fusion.2 = f32[512,2,1024]{2,0,1:T(8,128)} fusion(f32[512,1,1024]{2,0,1:T(8,128)S(1)} %bitcast_convert_fusion, f32[512,1,1024]{2,0,1:T(8,128)S(1)} %bitcast.16, pred[]{:T(512)S(6)} %eq.2), kind=kLoop, calls=%fused_computation.2 | loop fusion | flops 3145728 | bytes 8388609 | tf_op jit(solution)/shard_map/jit(_where)/select_n | solution.py:758
  206.0 5.4 %copy.12 = f32[512,2,1024]{0,2,1:T(8,128)} copy(f32[512,2,1024]{2,0,1:T(8,128)} %maximum_select_fusion.2) | data formatting | bytes 8388608 | tf_op jit(solution)/shard_map/jit(_where)/select_n | solution.py:758
  211.4 0.0 copy-start.3
  211.4 5.4 %copy.14 = f32[512,2048]{1,0:T(8,128)} copy(f32[512,2048]{0,1:T(8,128)} %bitcast.15) | data formatting | bytes 8388608
  216.8 0.0 copy-done.3
  216.8 1.0 copy.15
Async XLA Ops:
  193.4 7.0 %copy-start.1 = (f32[512,1024]{1,0:T(8,128)S(1)}, f32[512,1024]{1,0:T(8,128)}, u32[]{:S(2)}) copy-start(f32[512,1024]{1,0:T(8,128)} %get-tuple-element.32) | copy-start | bytes 6291460
  200.4 2.5 %copy-start.2 = (bf16[512,1024]{1,0:T(8,128)(2,1)S(1)}, bf16[512,1024]{1,0:T(8,128)(2,1)}, u32[]{:S(2)}) copy-start(bf16[512,1024]{1,0:T(8,128)(2,1)} %get-tuple-element.35) | copy-start | bytes 3145732
  200.4 3.1 %copy-start = (f32[512,1024]{1,0:T(8,128)S(1)}, f32[512,1024]{1,0:T(8,128)}, u32[]{:S(2)}) copy-start(f32[512,1024]{1,0:T(8,128)} %get-tuple-element.34) | copy-start | bytes 6291460
  211.4 5.4 %copy-start.3 = (bf16[256,1024]{1,0:T(8,128)(2,1)S(1)}, bf16[256,1024]{1,0:T(8,128)(2,1)}, u32[]{:S(2)}) copy-start(bf16[256,1024]{1,0:T(8,128)(2,1)} %get-tuple-element.36) | copy-start | bytes 1572868

commit v2 on v0

--- a/solution.py
+++ b/solution.py
@@ -1,6 +1,10 @@
+import functools
+
 import jax
 import jax.numpy as jnp
 from jax import lax
+from jax.experimental import pallas as pl
+from jax.experimental.pallas import tpu as pltpu
 from jax.sharding import PartitionSpec as P
 
 BLOCK = 1024
@@ -109,6 +113,686 @@
     return (first_out, new_left, new_right, direction, second_out)
 
 
+MESH = pl.DeviceIdType.MESH
+VMEM_LIMIT = 62 * 1024 * 1024
+PIECES = 4
+TILE = 256
+
+
+def remote(src, dst, send_sem, recv_sem, device):
+    return pltpu.make_async_remote_copy(
+        src_ref=src,
+        dst_ref=dst,
+        send_sem=send_sem,
+        recv_sem=recv_sem,
+        device_id=device,
+        device_id_type=MESH,
+    )
+
+
+def position():
+    return lax.axis_index("batch"), lax.axis_index("hidden"), lax.axis_index("solver")
+
+
+def flip(index, bits):
+    bit = 1
+    while bit <= bits:
+        if bits & bit:
+            index = index + bit * (1 - 2 * ((index // bit) % 2))
+        bit *= 2
+    return index
+
+
+def line_barrier(n_batch, n_line):
+    b, h, s = position()
+    barrier = pltpu.get_barrier_semaphore()
+    for bits in range(1, n_batch):
+        pl.semaphore_signal(barrier, inc=1, device_id=(flip(b, bits), h, s), device_id_type=MESH)
+    pl.semaphore_signal(barrier, inc=1, device_id=(b, h, 1 - s), device_id_type=MESH)
+
+    @pl.when(h > 0)
+    def _():
+        pl.semaphore_signal(barrier, inc=1, device_id=(b, h - 1, s), device_id_type=MESH)
+
+    @pl.when(h < n_line - 1)
+    def _():
+        pl.semaphore_signal(barrier, inc=1, device_id=(b, h + 1, s), device_id_type=MESH)
+
+    ends = (h == 0).astype(jnp.int32) + (h == n_line - 1).astype(jnp.int32)
+    pl.semaphore_wait(barrier, n_batch + 2 - ends)
+
+
+def tiles(count, step):
+    lax.fori_loop(0, count, lambda i, carry: (step(i), carry)[1], 0)
+
+
+def rows_at(i, size=TILE):
+    return pl.ds(pl.multiple_of(i * size, size), size)
+
+
+def dot(left, right):
+    return jnp.dot(left, right, preferred_element_type=jnp.float32)
+
+
+def update_statistics(old, left, right, own, sent, worst, s):
+    half = old.shape[0] // 2
+    worst[...] = jnp.zeros_like(worst)
+
+    def step(i):
+        at = rows_at(i)
+        new = STAT_DECAY * old[at, :] + (1.0 - STAT_DECAY) / BLOCK * dot(left[at, :], right[...])
+        old[at, :] = new
+        worst[...] = jnp.maximum(
+            worst[...], jnp.max(jnp.sum(jnp.abs(new), axis=1, keepdims=True), axis=0, keepdims=True)
+        )
+
+    tiles(old.shape[0] // TILE, step)
+
+    def split(i):
+        here = rows_at(i)
+        first = pl.multiple_of(s * half + i * TILE, TILE)
+        other = pl.multiple_of((1 - s) * half + i * TILE, TILE)
+        own[here, :] = old[pl.ds(first, TILE), :].astype(own.dtype)
+        sent[here, :] = old[pl.ds(other, TILE), :].astype(sent.dtype)
+
+    tiles(half // TILE, split)
+
+
+def series(stat, worst, step_one, step_two, step_three, tail, beside):
+    size = stat.shape[0]
+    scaled = 2.5 / (worst[...] + EPSILON)
+
+    def first(i):
+        at = rows_at(i)
+        row = lax.broadcasted_iota(jnp.int32, (TILE, size), 0) + i * TILE
+        col = lax.broadcasted_iota(jnp.int32, (TILE, size), 1)
+        diagonal = jnp.where(row == col, 0.25, 0.0)
+        step_one[at, :] = (diagonal - (0.25 * scaled) * stat[at, :]).astype(jnp.bfloat16)
+
+    tiles(size // TILE, first)
+
+    def second(i):
+        at = rows_at(i)
+        two = dot(step_one[at, :], step_one[...])
+        two_low = two.astype(jnp.bfloat16)
+        three = dot(two_low, step_one[...])
+        step_two[at, :] = two_low
+        step_three[at, :] = three.astype(jnp.bfloat16)
+        tail[at, :] = (8.75 * step_one[at, :].astype(jnp.float32) + 4.75 * two + three).astype(jnp.bfloat16)
+        beside(i)
+
+    tiles(size // TILE, second)
+    return jnp.sqrt(jnp.sqrt(scaled))
+
+
+def root_rows(at, step_one, step_two, step_three, tail):
+    f32 = jnp.float32
+    return (
+        step_one[at, :].astype(f32)
+        + 2.5 * step_two[at, :].astype(f32)
+        + 7.5 * step_three[at, :].astype(f32)
+        + dot(step_three[at, :], tail[...])
+    ).astype(jnp.bfloat16)
+
+
+class Reduction:
+    def __init__(self, n_batch, n_line, partial, out, inbox, from_above, from_below, sems):
+        self.n_batch, self.n_line = n_batch, n_line
+        self.partial, self.out, self.inbox = partial, out, inbox
+        self.from_above, self.from_below = from_above, from_below
+        self.local, self.swap_send, self.swap_recv, self.line_send, self.line_recv = sems
+        self.b, self.h, self.s = position()
+        self.tokens = out.shape[0]
+        self.rows = self.tokens // PIECES
+
+    def at(self, q):
+        return pl.ds(pl.multiple_of(q * self.rows, self.rows), self.rows)
+
+    def piece(self, bb, q):
+        return self.inbox.at[bb, self.at(q)]
+
+    def outgoing(self, bb, q):
+        return self.partial.at[pl.ds(pl.multiple_of(bb * self.tokens + q * self.rows, self.rows), self.rows)]
+
+    def own(self, q):
+        return pltpu.make_async_copy(self.outgoing(self.b, q), self.piece(self.b, q), self.local.at[q])
+
+    def swap(self, bits, q):
+        to = flip(self.b, bits)
+        return remote(
+            self.outgoing(to, q),
+            self.piece(self.b, q),
+            self.swap_send.at[bits, q],
+            self.swap_recv.at[bits, q],
+            (to, self.h, self.s),
+        )
+
+    def down_slot(self, bb, q):
+        return self.from_above.at[bb, self.at(q)]
+
+    def up_slot(self, bb, q):
+        return self.from_below.at[bb, self.at(q)]
+
+    def down(self, bb, q, source):
+        return remote(
+            source,
+            self.down_slot(bb, q),
+            self.line_send.at[bb, q],
+            self.line_recv.at[0, bb, q],
+            (self.b, self.h - 1, self.s),
+        )
+
+    def up(self, bb, q, source):
+        return remote(
+            source,
+            self.up_slot(bb, q),
+            self.line_send.at[bb, q],
+            self.line_recv.at[1, bb, q],
+            (self.b, self.h + 1, self.s),
+        )
+
+    def start(self):
+        half = self.n_batch // 2
+        for q in range(PIECES):
+            self.own(q).start()
+        for bits in [half + low for low in range(half)] + list(range(1, half)):
+            for q in range(PIECES):
+                self.swap(bits, q).start()
+
+    def arrive(self, bits, q):
+        if bits == 0:
+            self.own(q).wait()
+        else:
+            self.swap(bits, q).wait_recv()
+
+    def open(self, bits, q):
+        bb = flip(self.b, bits)
+
+        @pl.when((bb < self.h) & (self.h == self.n_line - 1))
+        def _():
+            self.arrive(bits, q)
+            self.down(bb, q, self.piece(bb, q)).start()
+
+        @pl.when((bb > self.h) & (self.h == 0))
+        def _():
+            self.arrive(bits, q)
+            self.up(bb, q, self.piece(bb, q)).start()
+
+    def relay(self, bits, q):
+        bb, h = flip(self.b, bits), self.h
+
+        @pl.when(bb == h)
+        def _():
+            self.arrive(bits, q)
+
+        def add(slot):
+            slot[...] = (
+                slot[...].astype(jnp.float32) + self.piece(bb, q)[...].astype(jnp.float32)
+            ).astype(slot.dtype)
+
+        @pl.when((bb < h) & (h < self.n_line - 1))
+        def _():
+            self.arrive(bits, q)
+            slot = self.down_slot(bb, q)
+            move = self.down(bb, q, slot)
+            move.wait_recv()
+            add(slot)
+            move.start()
+
+        @pl.when((bb > h) & (h > 0))
+        def _():
+            self.arrive(bits, q)
+            slot = self.up_slot(bb, q)
+            move = self.up(bb, q, slot)
+            move.wait_recv()
+            add(slot)
+            move.start()
+
+    def close(self, q):
+        h, out, at = self.h, self.out, self.at(q)
+        out[at, :] = self.piece(h, q)[...]
+
+        @pl.when(h < self.n_line - 1)
+        def _():
+            slot = self.down_slot(h, q)
+            self.down(h, q, slot).wait_recv()
+            out[at, :] = (out[at, :].astype(jnp.float32) + slot[...].astype(jnp.float32)).astype(out.dtype)
+
+        @pl.when(h > 0)
+        def _():
+            slot = self.up_slot(h, q)
+            self.up(h, q, slot).wait_recv()
+            out[at, :] = (out[at, :].astype(jnp.float32) + slot[...].astype(jnp.float32)).astype(out.dtype)
+
+    def sent(self, q):
+        for bits in range(1, self.n_batch):
+            self.swap(bits, q).wait_send()
+        for bb in range(self.n_line):
+            @pl.when(self.h > bb)
+            def _():
+                self.down(bb, q, self.down_slot(bb, q)).wait_send()
+
+            @pl.when(self.h < bb)
+            def _():
+                self.up(bb, q, self.up_slot(bb, q)).wait_send()
+
+
+def step_kernel(n_batch, n_line, *refs):
+    acts_ref, cot_ref, weight_ref, left_ref, right_ref = refs[0:5]
+    first_out, second_out = refs[5:7]
+    own_out, got_out = refs[7:10], refs[10:13]
+    acts_all, weight_all, cot_line, cot_all, grad, turned = refs[13:19]
+    left, right, one, two, three, tail, root = refs[19:26]
+    partials = refs[26:28]
+    inbox, from_above, from_below, own_rows, sent_rows, worst, squares = refs[28:35]
+    local_sem, acts_send, acts_recv, weight_send, weight_recv = refs[35:40]
+    line_send, line_recv, swap_send, swap_recv, swap_local = refs[40:45]
+    side_send, side_recv, own_sem = refs[45:48]
+    sums = refs[48:53]
+    b, h, s = position()
+    tokens, feats = acts_ref.shape
+    outs = cot_ref.shape[0]
+    rows = outs // PIECES
+    reductions = [
+        Reduction(
+            n_batch,
+            n_line,
+            partials[p],
+            (first_out, second_out)[p],
+            inbox.at[p],
+            from_above.at[p],
+            from_below.at[p],
+            [sem.at[p] for sem in sums],
+        )
+        for p in range(2)
+    ]
+
+    def acts_slot(bb, ss):
+        return acts_all.at[
+            pl.ds(pl.multiple_of(bb * tokens, tokens), tokens),
+            pl.ds(pl.multiple_of(ss * feats, feats), feats),
+        ]
+
+    def weight_from(ss):
+        return weight_ref.at[:, pl.ds(pl.multiple_of(ss * outs, outs), outs)]
+
+    def weight_slot(ss):
+        return weight_all.at[pl.ds(pl.multiple_of(ss * feats, feats), feats), :]
+
+    own_cot = pltpu.make_async_copy(cot_ref, cot_line.at[h], local_sem.at[0])
+    own_acts = pltpu.make_async_copy(acts_ref, acts_slot(b, s), local_sem.at[1])
+    own_weight = pltpu.make_async_copy(weight_from(s), weight_slot(s), local_sem.at[2])
+    left_in = pltpu.make_async_copy(left_ref.at[0, s], left, local_sem.at[3])
+    right_in = pltpu.make_async_copy(right_ref.at[0, s], right, local_sem.at[4])
+    own_cot.start()
+    own_acts.start()
+    line_barrier(n_batch, n_line)
+    own_weight.start()
+    right_in.start()
+    left_in.start()
+    own_acts.wait()
+    own_cot.wait()
+
+    def line_slot(hp, q):
+        return cot_line.at[hp, pl.ds(q * rows, rows)]
+
+    def up(hp, q):
+        return remote(
+            line_slot(hp, q), line_slot(hp, q), line_send.at[0, hp, q], line_recv.at[hp, q], (b, h + 1, s)
+        )
+
+    def down(hp, q):
+        return remote(
+            line_slot(hp, q), line_slot(hp, q), line_send.at[1, hp, q], line_recv.at[hp, q], (b, h - 1, s)
+        )
+
+    def swap_slot(bb, q):
+        return cot_all.at[rows_at(q, rows), pl.ds(pl.multiple_of(bb * tokens, tokens), tokens)]
+
+    def swap(hp, q):
+        return remote(
+            line_slot(hp, q), swap_slot(b, q), swap_send.at[hp, q], swap_recv.at[b, q], (hp, h, s)
+        )
+
+    def swap_here(q):
+        return pltpu.make_async_copy(
+            cot_line.at[b, rows_at(q, rows)], swap_slot(b, q), swap_local.at[q]
+        )
+
+    def pass_on(hp, q):
+        @pl.when(hp == b)
+        def _():
+            swap_here(q).start()
+
+        @pl.when(hp != b)
+        def _():
+            swap(hp, q).start()
+
+    far = n_batch // 2
+    acts_moves = []
+
+    def acts_move(bb, ss, device):
+        index = len(acts_moves)
+        move = remote(
+            acts_slot(bb, ss), acts_slot(bb, ss), acts_send.at[index], acts_recv.at[bb, ss], device
+        )
+        move.start()
+        acts_moves.append(move)
+
+    def acts_wait(bb, ss):
+        remote(acts_slot(bb, ss), acts_slot(bb, ss), acts_send.at[0], acts_recv.at[bb, ss], (b, h, s)).wait_recv()
+
+    acts_move(b, s, (flip(b, far), h, s))
+    acts_move(b, s, (b, h, 1 - s))
+    for q in range(PIECES):
+        @pl.when(h < n_line - 1)
+        def _():
+            up(h, q).start()
+
+        @pl.when(h > 0)
+        def _():
+            down(h, q).start()
+
+    near = [bits for bits in range(1, far)]
+    for bits in near:
+        acts_move(b, s, (flip(b, bits), h, s))
+    for q in range(PIECES):
+        pass_on(h, q)
+    acts_wait(flip(b, far), s)
+    acts_move(flip(b, far), s, (b, h, 1 - s))
+    for bits in near:
+        acts_move(flip(b, far), s, (flip(b, bits), h, s))
+    weight_move = remote(weight_from(1 - s), weight_slot(s), weight_send, weight_recv, (b, h, 1 - s))
+    weight_move.start()
+    for place in (b, flip(b, far)):
+        acts_wait(place, 1 - s)
+        for bits in near:
+            acts_move(place, 1 - s, (flip(b, bits), h, s))
+
+    for distance in range(1, n_line):
+        for q in range(PIECES):
+            @pl.when(h >= distance)
+            def _():
+                hp = h - distance
+                up(hp, q).wait_recv()
+
+                @pl.when(h < n_line - 1)
+                def _():
+                    up(hp, q).start()
+
+                pass_on(hp, q)
+
+            @pl.when(h + distance < n_line)
+            def _():
+                hp = h + distance
+                down(hp, q).wait_recv()
+
+                @pl.when(h > 0)
+                def _():
+                    down(hp, q).start()
+
+                pass_on(hp, q)
+
+    for bits in near:
+        for place in (flip(b, bits), flip(b, bits + far)):
+            for ss in range(2):
+                acts_wait(place, ss)
+    own_weight.wait()
+    weight_move.wait_recv()
+
+    def forward(partial, block_weight):
+        def step(i):
+            at = rows_at(i)
+            partial[at, :] = dot(acts_all[at, :], block_weight[...]).astype(jnp.bfloat16)
+
+        tiles(acts_all.shape[0] // TILE, step)
+
+    forward(partials[0], weight_all)
+    first, second = reductions
+    first.start()
+
+    def early(q):
+        first.open(0, q)
+        first.open(1, q)
+
+    tiles(PIECES, early)
+
+    def grad_rows(q):
+        swap_here(q).wait()
+        for bits in range(1, n_batch):
+            place = flip(b, bits)
+            remote(
+                swap_slot(place, q), swap_slot(place, q), swap_send.at[0, q], swap_recv.at[place, q], (b, h, s)
+            ).wait_recv()
+        at = rows_at(q, rows)
+        value = dot(cot_all[at, :], acts_all[...]).astype(jnp.bfloat16)
+        grad[at, :] = value
+        turned[:, at] = value.T
+
+    tiles(PIECES, grad_rows)
+
+    own_moves, side_moves = [], []
+
+    def exchange(i):
+        own = pltpu.make_async_copy(own_rows.at[i], own_out[i], own_sem.at[i])
+        side = remote(sent_rows.at[i], got_out[i], side_send.at[i], side_recv.at[i], (b, h, 1 - s))
+        own.start()
+        side.start()
+        own_moves.append(own)
+        side_moves.append(side)
+
+    right_in.wait()
+    update_statistics(right, grad, turned, own_rows.at[1], sent_rows.at[1], worst, s)
+    exchange(1)
+
+    def beside_right(q):
+        first.open(2, q)
+        first.relay(0, q)
+
+    scale_right = series(right, worst, one, two, three, tail, beside_right)
+
+    def right_root(i):
+        root[rows_at(i), :] = root_rows(rows_at(i), one, two, three, tail)
+
+    tiles(BLOCK // TILE, right_root)
+
+    left_in.wait()
+    update_statistics(left, turned, grad, own_rows.at[0], sent_rows.at[0], worst, s)
+    exchange(0)
+
+    def beside_left(q):
+        first.open(3, q)
+        first.relay(1, q)
+
+    scale = series(left, worst, one, two, three, tail, beside_left) * scale_right
+    squares[...] = jnp.zeros_like(squares)
+    update = left
+
+    def apply(i):
+        at = rows_at(i)
+        left_rows = root_rows(at, one, two, three, tail)
+        mixed = turned[at, :].astype(jnp.float32) + dot(left_rows, turned[...])
+        value = mixed + dot(mixed.astype(jnp.bfloat16), root[...])
+        update[at, :] = value
+        squares[...] += jnp.sum(jnp.sum(value * value, axis=1, keepdims=True), axis=0, keepdims=True)
+        first.relay(2, i)
+
+    tiles(BLOCK // TILE, apply)
+    scaled = scale / jnp.sqrt(scale * scale * squares[...] / (BLOCK * BLOCK) + EPSILON)
+    half = BLOCK // 2
+
+    def finish(i):
+        at = rows_at(i)
+        root[at, :] = (
+            weight_all[at, :].astype(jnp.float32) - LEARN_RATE * (scaled * update[at, :])
+        ).astype(jnp.bfloat16)
+
+    tiles(BLOCK // TILE, finish)
+    forward(partials[1], root)
+    second.start()
+
+    def split(i):
+        here = rows_at(i)
+        mine = pl.multiple_of(s * half + i * TILE, TILE)
+        other = pl.multiple_of((1 - s) * half + i * TILE, TILE)
+        own_rows[2, here, :] = (scaled * update[pl.ds(mine, TILE), :]).astype(jnp.bfloat16)
+        sent_rows[2, here, :] = (scaled * update[pl.ds(other, TILE), :]).astype(jnp.bfloat16)
+
+    tiles(half // TILE, split)
+    exchange(2)
+
+    tiles(PIECES, lambda q: first.relay(3, q))
+    for bits in range(n_batch):
+        def both(q):
+            second.open(bits, q)
+            second.relay(bits, q)
+
+        tiles(PIECES, both)
+    tiles(PIECES, first.close)
+    tiles(PIECES, second.close)
+
+    for move in acts_moves:
+        move.wait_send()
+    weight_move.wait_send()
+    for hp in range(n_line):
+        for q in range(PIECES):
+            @pl.when((hp <= h) & (h < n_line - 1))
+            def _():
+                up(hp, q).wait_send()
+
+            @pl.when((hp >= h) & (h > 0))
+            def _():
+                down(hp, q).wait_send()
+
+            @pl.when(hp != b)
+            def _():
+                swap(hp, q).wait_send()
+    for reduction in reductions:
+        tiles(PIECES, reduction.sent)
+    for move in own_moves:
+        move.wait()
+    for move in side_moves:
+        move.wait()
+
+
+def block_step(activations, cotangent, weight, left_old, right_old, n_batch, n_line):
+    tokens, feats = activations.shape
+    outs = cotangent.shape[0]
+    all_tokens, half = n_batch * tokens, BLOCK // 2
+    vmem = pl.BlockSpec(memory_space=pltpu.VMEM)
+    hbm = pl.BlockSpec(memory_space=pl.ANY)
+    sem = pltpu.SemaphoreType.DMA
+    bf, f32 = jnp.bfloat16, jnp.float32
+    out = jax.ShapeDtypeStruct((tokens, outs), bf)
+    part = jax.ShapeDtypeStruct((half, BLOCK), bf)
+    low, wide = pltpu.VMEM((BLOCK, BLOCK), bf), pltpu.VMEM((BLOCK, BLOCK), f32)
+    partial = pltpu.VMEM((all_tokens, outs), bf)
+    return pl.pallas_call(
+        functools.partial(step_kernel, n_batch, n_line),
+        out_shape=(out, out) + (part,) * 6,
+        in_specs=[hbm] * 5,
+        out_specs=(vmem,) * 2 + (hbm,) * 6,
+        scratch_shapes=[
+            pltpu.VMEM((all_tokens, BLOCK), bf),
+            low,
+            pltpu.VMEM((n_line, outs, tokens), bf),
+            pltpu.VMEM((outs, all_tokens), bf),
+            low,
+            low,
+            wide,
+            wide,
+            low,
+            low,
+            low,
+            low,
+            low,
+            partial,
+            partial,
+            pltpu.VMEM((2, n_batch, tokens, outs), bf),
+            pltpu.VMEM((2, n_line, tokens, outs), bf),
+            pltpu.VMEM((2, n_line, tokens, outs), bf),
+            pltpu.VMEM((3, half, BLOCK), bf),
+            pltpu.VMEM((3, half, BLOCK), bf),
+            pltpu.VMEM((1, 1), f32),
+            pltpu.VMEM((1, 1), f32),
+            sem((5,)),
+            sem((2 * n_batch - 1,)),
+            sem((n_batch, 2)),
+            sem,
+            sem,
+            sem((2, n_line, PIECES)),
+            sem((n_line, PIECES)),
+            sem((n_line, PIECES)),
+            sem((n_batch, PIECES)),
+            sem((PIECES,)),
+            sem((3,)),
+            sem((3,)),
+            sem((3,)),
+            sem((2, PIECES)),
+            sem((2, n_batch, PIECES)),
+            sem((2, n_batch, PIECES)),
+            sem((2, n_line, PIECES)),
+            sem((2, 2, n_line, PIECES)),
+        ],
+        compiler_params=pltpu.CompilerParams(
+            collective_id=0, has_side_effects=True, vmem_limit_bytes=VMEM_LIMIT
+        ),
+        name="block_step",
+    )(activations, cotangent, weight, left_old, right_old)
+
+
+ASSEMBLE_STEPS = 4
+
+
+def assemble_kernel(
+    left_own, right_own, direction_own, left_got, right_got, direction_got, first_in, second_in,
+    first, left, right, direction, second,
+):
+    s = lax.axis_index("solver")
+    width = direction_own.shape[1]
+    for own, got, out in ((left_own, left_got, left), (right_own, right_got, right)):
+        out[0, s] = own[...].astype(jnp.float32)
+        out[0, 1 - s] = got[...].astype(jnp.float32)
+    direction[:, pl.ds(pl.multiple_of(s * width, width), width)] = direction_own[...].astype(jnp.float32)
+    direction[:, pl.ds(pl.multiple_of((1 - s) * width, width), width)] = direction_got[...].astype(jnp.float32)
+    first[...] = first_in[...].T
+    second[...] = second_in[...].T
+
+
+def assemble(rows, first, second):
+    half, width = rows[0].shape
+    tokens, outs = first.shape
+    step = half // ASSEMBLE_STEPS
+    cols = outs // ASSEMBLE_STEPS
+    f32 = jnp.float32
+    part = pl.BlockSpec((step, width), lambda i: (i, 0))
+    stat = pl.BlockSpec((1, 2, step, width), lambda i: (0, 0, i, 0))
+    turned_in = pl.BlockSpec((tokens, cols), lambda i: (0, i))
+    turned_out = pl.BlockSpec((cols, tokens), lambda i: (i, 0))
+    return pl.pallas_call(
+        assemble_kernel,
+        grid=(ASSEMBLE_STEPS,),
+        out_shape=(
+            jax.ShapeDtypeStruct((outs, tokens), first.dtype),
+            jax.ShapeDtypeStruct((1, 2, half, width), f32),
+            jax.ShapeDtypeStruct((1, 2, half, width), f32),
+            jax.ShapeDtypeStruct((half, 2 * width), f32),
+            jax.ShapeDtypeStruct((outs, tokens), first.dtype),
+        ),
+        in_specs=[part] * 6 + [turned_in] * 2,
+        out_specs=(turned_out, stat, stat, pl.BlockSpec((step, 2 * width), lambda i: (i, 0)), turned_out),
+        compiler_params=pltpu.CompilerParams(vmem_limit_bytes=VMEM_LIMIT),
+        name="assemble",
+    )(*rows, first, second)
+
+
+def owned_body(activations, cotangent, weight, left_old, right_old, *, n_batch, n_line):
+    first, second, *rows = block_step(
+        activations, cotangent, weight, left_old, right_old, n_batch, n_line
+    )
+    return assemble(rows, first, second)
+
+
 def solution(mesh):
     in_specs = (
         P("batch", ("hidden", "solver")),
@@ -127,7 +811,18 @@
     n_batch = mesh.shape["batch"]
     n_feat = mesh.shape["hidden"] * mesh.shape["solver"]
 
+    n_line = mesh.shape["hidden"]
+    n_solver = mesh.shape["solver"]
+
+    def owned(activations, cotangent, weight, left_old, right_old):
+        blocks = left_old.shape[1]
+        even = n_line == n_batch == 2 * n_solver
+        return even and n_solver == 2 and blocks == n_solver and cotangent.shape[0] == BLOCK
+
     def step(activations, cotangent, weight, left_old, right_old):
+        args = (activations, cotangent, weight, left_old, right_old)
+        if owned(*args):
+            return owned_body(*args, n_batch=n_batch, n_line=n_line)
         return body(
             activations,
             cotangent,

time: 420 us -> 163 us (0.39)
  the two profiles are of different devices: /device:TPU:4 before, /device:TPU:24 now
where the time goes in v2:
time: 163 us; the launch traced here: 162 us
  Pallas kernels  162 us (99%)
    pallas_call x1, Pallas kernels, block_step(): pl.pallas_call(functools.partial(step_kernel, n_batch, n_line), out_shape...  153 us
    pallas_call x1, Pallas kernels, assemble(): pl.pallas_call(assemble_kernel, grid=(ASSEMBLE_STEPS,), out_shape=(jax.Sh...  8.49 us

profile of v2, /device:TPU:24, one launch (start us, length us, event | category | flops | bytes accessed | tf_op | source)
XLA Modules:
  0.0 162.5 jit_solution(5130829508366577953)
XLA Ops:
  0.6 153.4 %block_step.1 = (bf16[256,1024]{1,0:T(8,128)(2,1)}, bf16[256,1024]{1,0:T(8,128)(2,1)}, bf16[512,1024]{1,0:T(8,128)(2,1)}, bf16[512,1024]{1,0:T(8,128)(2,1)}, bf1...) custom-call(bf16[256,512]{1,0:T(8,128)(2,1)} %refs_0_.1, ...), custom_call_target="tpu_custom_call" | custom-call | tf_op jit(solution)/shard_map/block_step/pallas_call | solution.py:690
  154.0 8.5 %assemble.1 = (bf16[1024,256]{1,0:T(8,128)(2,1)}, f32[1,2,512,1024]{3,2,1,0:T(8,128)}, f32[1,2,512,1024]{3,2,1,0:T(8,128)}, f32[512,2048]{1,0:T(8,128)}, bf16[1024,256]{1,0:T(8,128)(2,1)}) custom-call(bf16[512,1024]{1,0:T(8,128)(2,1)} %get-tuple-element.13.left_own, bf16[512,1024]{1,0:T(8,128)(2,1)} %get-tuple-element.14.right_own, ...), custom_call_target="tpu_custom_call" | custom-call | tf_op jit(solution)/shard_map/assemble/pallas_call | solution.py:772

commit v3 on v2

--- a/solution.py
+++ b/solution.py
@@ -116,7 +116,7 @@
 MESH = pl.DeviceIdType.MESH
 VMEM_LIMIT = 62 * 1024 * 1024
 PIECES = 4
-TILE = 256
+TILE = 512
 
 
 def remote(src, dst, send_sem, recv_sem, device):
@@ -174,7 +174,7 @@
     return jnp.dot(left, right, preferred_element_type=jnp.float32)
 
 
-def update_statistics(old, left, right, own, sent, worst, s):
+def update_statistics(old, left, right, own, sent, worst, s, beside):
     half = old.shape[0] // 2
     worst[...] = jnp.zeros_like(worst)
 
@@ -185,6 +185,7 @@
         worst[...] = jnp.maximum(
             worst[...], jnp.max(jnp.sum(jnp.abs(new), axis=1, keepdims=True), axis=0, keepdims=True)
         )
+        beside(i)
 
     tiles(old.shape[0] // TILE, step)
 
@@ -299,53 +300,74 @@
             for q in range(PIECES):
                 self.swap(bits, q).start()
 
+    def down_target(self, step):
+        half = self.n_batch // 2
+        high, low = self.b // half, self.b % half
+        other = step ^ half
+        return flip(low, step), step + high * (other - step)
+
+    def up_target(self, step):
+        half = self.n_batch // 2
+        high, low = self.b // half, self.b % half
+        other = step ^ half
+        return flip(low + half, step), other + high * (step - other)
+
     def arrive(self, bits, q):
-        if bits == 0:
+        @pl.when(bits == 0)
+        def _():
             self.own(q).wait()
-        else:
-            self.swap(bits, q).wait_recv()
-
-    def open(self, bits, q):
-        bb = flip(self.b, bits)
-
-        @pl.when((bb < self.h) & (self.h == self.n_line - 1))
+
+        @pl.when(bits != 0)
+        def _():
+            slot = self.piece(self.b, q)
+            place = (self.b, self.h, self.s)
+            remote(slot, slot, self.swap_send.at[bits, q], self.swap_recv.at[bits, q], place).wait_recv()
+
+    def open(self, step, q):
+        target, bits = self.down_target(step)
+
+        @pl.when((target < self.h) & (self.h == self.n_line - 1))
         def _():
             self.arrive(bits, q)
-            self.down(bb, q, self.piece(bb, q)).start()
-
-        @pl.when((bb > self.h) & (self.h == 0))
+            self.down(target, q, self.piece(target, q)).start()
+
+        over, over_bits = self.up_target(step)
+
+        @pl.when((over > self.h) & (self.h == 0))
+        def _():
+            self.arrive(over_bits, q)
+            self.up(over, q, self.piece(over, q)).start()
+
+    def relay(self, step, q):
+        h = self.h
+        target, bits = self.down_target(step)
+        over, over_bits = self.up_target(step)
+
+        def add(slot, owner):
+            slot[...] = (
+                slot[...].astype(jnp.float32) + self.piece(owner, q)[...].astype(jnp.float32)
+            ).astype(slot.dtype)
+
+        @pl.when(target == h)
         def _():
             self.arrive(bits, q)
-            self.up(bb, q, self.piece(bb, q)).start()
-
-    def relay(self, bits, q):
-        bb, h = flip(self.b, bits), self.h
-
-        @pl.when(bb == h)
+
+        @pl.when((target < h) & (h < self.n_line - 1))
         def _():
             self.arrive(bits, q)
-
-        def add(slot):
-            slot[...] = (
-                slot[...].astype(jnp.float32) + self.piece(bb, q)[...].astype(jnp.float32)
-            ).astype(slot.dtype)
-
-        @pl.when((bb < h) & (h < self.n_line - 1))
-        def _():
-            self.arrive(bits, q)
-            slot = self.down_slot(bb, q)
-            move = self.down(bb, q, slot)
+            slot = self.down_slot(target, q)
+            move = self.down(target, q, slot)
             move.wait_recv()
-            add(slot)
+            add(slot, target)
             move.start()
 
-        @pl.when((bb > h) & (h > 0))
-        def _():
-            self.arrive(bits, q)
-            slot = self.up_slot(bb, q)
-            move = self.up(bb, q, slot)
+        @pl.when((over > h) & (h > 0))
+        def _():
+            self.arrive(over_bits, q)
+            slot = self.up_slot(over, q)
+            move = self.up(over, q, slot)
             move.wait_recv()
-            add(slot)
+            add(slot, over)
             move.start()
 
     def close(self, q):
@@ -385,6 +407,7 @@
     left, right, one, two, three, tail, root = refs[19:26]
     partials = refs[26:28]
     inbox, from_above, from_below, own_rows, sent_rows, worst, squares = refs[28:35]
+    worst_right = refs[53]
     local_sem, acts_send, acts_recv, weight_send, weight_recv = refs[35:40]
     line_send, line_recv, swap_send, swap_recv, swap_local = refs[40:45]
     side_send, side_recv, own_sem = refs[45:48]
@@ -551,12 +574,6 @@
     first, second = reductions
     first.start()
 
-    def early(q):
-        first.open(0, q)
-        first.open(1, q)
-
-    tiles(PIECES, early)
-
     def grad_rows(q):
         swap_here(q).wait()
         for bits in range(1, n_batch):
@@ -581,30 +598,42 @@
         own_moves.append(own)
         side_moves.append(side)
 
+    def pieces(i):
+        per = PIECES * TILE // BLOCK
+        return [i * per + q for q in range(per)]
+
+    def beside_right(i):
+        first.open(0, i)
+
+    def beside_left(i):
+        first.open(0, PIECES // 2 + i)
+
     right_in.wait()
-    update_statistics(right, grad, turned, own_rows.at[1], sent_rows.at[1], worst, s)
+    update_statistics(right, grad, turned, own_rows.at[1], sent_rows.at[1], worst_right, s, beside_right)
     exchange(1)
-
-    def beside_right(q):
-        first.open(2, q)
-        first.relay(0, q)
-
-    scale_right = series(right, worst, one, two, three, tail, beside_right)
+    left_in.wait()
+    update_statistics(left, turned, grad, own_rows.at[0], sent_rows.at[0], worst, s, beside_left)
+    exchange(0)
+
+    def right_powers(i):
+        first.open(1, i)
+        for q in pieces(i):
+            first.relay(0, q)
+
+    scale_right = series(right, worst_right, one, two, three, tail, right_powers)
 
     def right_root(i):
         root[rows_at(i), :] = root_rows(rows_at(i), one, two, three, tail)
+        first.open(1, PIECES // 2 + i)
 
     tiles(BLOCK // TILE, right_root)
 
-    left_in.wait()
-    update_statistics(left, turned, grad, own_rows.at[0], sent_rows.at[0], worst, s)
-    exchange(0)
-
-    def beside_left(q):
-        first.open(3, q)
-        first.relay(1, q)
-
-    scale = series(left, worst, one, two, three, tail, beside_left) * scale_right
+    def left_powers(i):
+        for q in pieces(i):
+            first.open(2, q)
+            first.relay(1, q)
+
+    scale = series(left, worst, one, two, three, tail, left_powers) * scale_right
     squares[...] = jnp.zeros_like(squares)
     update = left
 
@@ -615,7 +644,9 @@
         value = mixed + dot(mixed.astype(jnp.bfloat16), root[...])
         update[at, :] = value
         squares[...] += jnp.sum(jnp.sum(value * value, axis=1, keepdims=True), axis=0, keepdims=True)
-        first.relay(2, i)
+        for q in pieces(i):
+            first.open(3, q)
+            first.relay(2, q)
 
     tiles(BLOCK // TILE, apply)
     scaled = scale / jnp.sqrt(scale * scale * squares[...] / (BLOCK * BLOCK) + EPSILON)
@@ -642,10 +673,10 @@
     exchange(2)
 
     tiles(PIECES, lambda q: first.relay(3, q))
-    for bits in range(n_batch):
+    for step in range(n_batch):
         def both(q):
-            second.open(bits, q)
-            second.relay(bits, q)
+            second.open(step, q)
+            second.relay(step, q)
 
         tiles(PIECES, both)
     tiles(PIECES, first.close)
@@ -733,6 +764,7 @@
             sem((2, n_batch, PIECES)),
             sem((2, n_line, PIECES)),
             sem((2, 2, n_line, PIECES)),
+            pltpu.VMEM((1, 1), f32),
         ],
         compiler_params=pltpu.CompilerParams(
             collective_id=0, has_side_effects=True, vmem_limit_bytes=VMEM_LIMIT
@@ -741,7 +773,7 @@
     )(activations, cotangent, weight, left_old, right_old)
 
 
-ASSEMBLE_STEPS = 4
+ASSEMBLE_STEPS = 2
 
 
 def assemble_kernel(

time: 163 us -> 141 us (0.87)
  Pallas kernels: 162 us -> 140 us
    pallas_call x1, Pallas kernels: 153 us -> 132 us  [block_step(): pl.pallas_call(functools.partial(step_kernel, n_batch, n_line), out_shape...]
where the time goes in v3:
time: 141 us
  Pallas kernels  140 us (99%)
    pallas_call x1, Pallas kernels, block_step(): pl.pallas_call(functools.partial(step_kernel, n_batch, n_line), out_shape...  132 us
    pallas_call x1, Pallas kernels, assemble(): pl.pallas_call(assemble_kernel, grid=(ASSEMBLE_STEPS,), out_shape=(jax.Sh...  7.31 us

profile of v3, /device:TPU:24, one launch (start us, length us, event | category | flops | bytes accessed | tf_op | source)
XLA Modules:
  0.0 140.6 jit_solution(9143355731367066788)
XLA Ops:
  0.6 132.5 %block_step.1 = (bf16[256,1024]{1,0:T(8,128)(2,1)}, bf16[256,1024]{1,0:T(8,128)(2,1)}, bf16[512,1024]{1,0:T(8,128)(2,1)}, bf16[512,1024]{1,0:T(8,128)(2,1)}, bf1...) custom-call(bf16[256,512]{1,0:T(8,128)(2,1)} %refs_0_.1, ...), custom_call_target="tpu_custom_call" | custom-call | tf_op jit(solution)/shard_map/block_step/pallas_call | solution.py:721
  133.1 7.3 %assemble.1 = (bf16[1024,256]{1,0:T(8,128)(2,1)}, f32[1,2,512,1024]{3,2,1,0:T(8,128)}, f32[1,2,512,1024]{3,2,1,0:T(8,128)}, f32[512,2048]{1,0:T(8,128)}, bf16[1024,256]{1,0:T(8,128)(2,1)}) custom-call(bf16[512,1024]{1,0:T(8,128)(2,1)} %get-tuple-element.13.left_own, bf16[512,1024]{1,0:T(8,128)(2,1)} %get-tuple-element.14.right_own, ...), custom_call_target="tpu_custom_call" | custom-call | tf_op jit(solution)/shard_map/assemble/pallas_call | solution.py:804

commit v4 on v3

--- a/solution.py
+++ b/solution.py
@@ -617,13 +617,13 @@
 
     def right_powers(i):
         first.open(1, i)
+
+    scale_right = series(right, worst_right, one, two, three, tail, right_powers)
+
+    def right_root(i):
+        root[rows_at(i), :] = root_rows(rows_at(i), one, two, three, tail)
         for q in pieces(i):
             first.relay(0, q)
-
-    scale_right = series(right, worst_right, one, two, three, tail, right_powers)
-
-    def right_root(i):
-        root[rows_at(i), :] = root_rows(rows_at(i), one, two, three, tail)
         first.open(1, PIECES // 2 + i)
 
     tiles(BLOCK // TILE, right_root)

time: 141 us -> 144 us (1.021)
  Pallas kernels: 140 us -> 142 us
    pallas_call x1, Pallas kernels: 132 us -> 134 us  [block_step(): pl.pallas_call(functools.partial(step_kernel, n_batch, n_line), out_shape...]
where the time goes in v4:
time: 144 us; the launch traced here: 142 us
  Pallas kernels  142 us (99%)
    pallas_call x1, Pallas kernels, block_step(): pl.pallas_call(functools.partial(step_kernel, n_batch, n_line), out_shape...  134 us
    pallas_call x1, Pallas kernels, assemble(): pl.pallas_call(assemble_kernel, grid=(ASSEMBLE_STEPS,), out_shape=(jax.Sh...  7.31 us

profile of v4, /device:TPU:24, one launch (start us, length us, event | category | flops | bytes accessed | tf_op | source)
XLA Modules:
  0.0 142.4 jit_solution(4310354581178373324)
XLA Ops:
  0.6 134.3 %block_step.1 = (bf16[256,1024]{1,0:T(8,128)(2,1)}, bf16[256,1024]{1,0:T(8,128)(2,1)}, bf16[512,1024]{1,0:T(8,128)(2,1)}, bf16[512,1024]{1,0:T(8,128)(2,1)}, bf1...) custom-call(bf16[256,512]{1,0:T(8,128)(2,1)} %refs_0_.1, ...), custom_call_target="tpu_custom_call" | custom-call | tf_op jit(solution)/shard_map/block_step/pallas_call | solution.py:721
  134.9 7.3 %assemble.1 = (bf16[1024,256]{1,0:T(8,128)(2,1)}, f32[1,2,512,1024]{3,2,1,0:T(8,128)}, f32[1,2,512,1024]{3,2,1,0:T(8,128)}, f32[512,2048]{1,0:T(8,128)}, bf16[1024,256]{1,0:T(8,128)(2,1)}) custom-call(bf16[512,1024]{1,0:T(8,128)(2,1)} %get-tuple-element.13.left_own, bf16[512,1024]{1,0:T(8,128)(2,1)} %get-tuple-element.14.right_own, ...), custom_call_target="tpu_custom_call" | custom-call | tf_op jit(solution)/shard_map/assemble/pallas_call | solution.py:804
